TPU v7x, 512 devices: a whole 4x8x8 slice. The times are simulated.
512 devices in a mesh: ctx: 64 (over z_lo, y, core), head: 8 (over x, z_hi).
Axes of the slice: x: 4, y: 8, z: 8 (z_hi: 2, z_lo: 4; z = z_hi * 4 + z_lo), core: 2. Of those that a mesh axis runs over, the one named last changes fastest.
Arguments:
- tokens: bfloat16 [32768, 3840], P('ctx', 'head'), may hold values from -18 to 18
- w_query: bfloat16 [3840, 4096], P('ctx', 'head'), may hold values from -0.09375 to 0.09375
- key_matrix: bfloat16 [3840, 2048], P('ctx', 'head'), may hold values from -0.09375 to 0.09375
- value_matrix: bfloat16 [3840, 2048], P('ctx', 'head'), may hold values from -0.09375 to 0.09375
- d_attended: bfloat16 [32768, 4096], P('ctx', 'head'), may hold values from -6 to 6
- doc_lengths: int32 [32], replicated, may hold values from 1 to 2048, 32768 in all
Outputs:
- attended: bfloat16 [32768, 4096], P('ctx', 'head')
- key_grad: bfloat16 [32768, 2048], P('ctx', 'head')
Inputs may be any that keep to these rules, and one draw needn't show every extreme that they name: `doc_lengths`: the documents lie end to end from position 0 and fill all 32768 positions.
All inputs are finite; a program needn't handle non-finite values.
Results may differ from a plain program's by a relative error of at most 0.012.
The roundings to bfloat16 on the way count: a program that leaves them out, or rounds other values in their place, can miss the bound.
Values may be sent and summed in bfloat16 or wider, within the bound.
No kernel may reach another device: no remote copies, remote signals or barrier semaphores. Data moves between devices by JAX's collectives and lax.ppermute only.
A program may use at most 64 MiB of HBM per device.

v0:
```python
import jax
import jax.numpy as jnp
from jax import lax
from jax.experimental import pallas as pl
from jax.experimental.pallas import tpu as pltpu
from jax.sharding import PartitionSpec as P


HEAD_SIZE = 256
WINDOW = 1024
NX, NY, NZL, NZH = 4, 8, 4, 2
NZ = NZL * NZH
ROWS = 60
PAD = 64
PAIR = 2 * PAD
BOTH = ("ctx", "head")
BF = jnp.bfloat16
F32 = jnp.float32
MIB = 1024 * 1024


def place(x, y, z, core):
    x, y, z = x % NX, y % NY, z % NZ
    ctx = (z % NZL) * 2 * NY + 2 * y + core
    return ctx * (NX * NZH) + x * NZH + z // NZL


def hop(block, dx=0, dy=0, dz=0, swap=0, by_core=False, flip=0):
    route = []
    for x in range(NX):
        for y in range(NY):
            for z in range(NZ):
                for core in range(2):
                    s = 1 - 2 * core if by_core else 1
                    route.append(
                        (
                            place(x, y, z, core),
                            place(x + s * dx, y + s * dy, (z ^ flip) + s * dz, core ^ swap),
                        )
                    )
    return lax.ppermute(block, BOTH, route)


def along_ctx(block, distance):
    n = lax.axis_size("ctx")
    route = [(i - distance, i) for i in range(n) if 0 <= i - distance < n]
    return lax.ppermute(block, "ctx", route)


def project_body(t0, t1, t2, t3, p0, p1, p2, p3, own_ref, r1, r2, r3, r4, swapped, o_ref, *, scale):
    ctx = lax.axis_index("ctx").astype(jnp.int32)
    head = lax.axis_index("head").astype(jnp.int32)
    y = lax.rem(lax.div(ctx, 2), NY)
    own_z = lax.div(ctx, 2 * NY)
    sign = 1 - 2 * lax.rem(ctx, 2)
    x, zh = lax.div(head, NZH), lax.rem(head, NZH)
    total = jnp.zeros(o_ref.shape, F32)

    for slot, (near, far) in enumerate(((t0, p0), (t1, p1), (t2, p2), (t3, p3))):
        z = lax.rem(x - sign * slot + NX, NX)

        def columns(distance):
            chip = lax.rem(y + sign * distance + NY, NY)
            at = pl.multiple_of(lax.rem(chip, 4) * PAIR, PAIR)
            return jnp.where(lax.div(chip, 4) == zh, near[:, pl.ds(at, PAIR)], far[:, pl.ds(at, PAIR)])

        left = [columns(d) for d in (0, 4, -1, 1, -2, 2, -3, 3)]
        j = lax.bitwise_xor(z, own_z)
        right = [own_ref[j], own_ref[NZL + j], r4[j], r4[NZL + j]]
        for step, ref in enumerate((r1, r2, r3)):
            at = 2 * NZL * step + j
            right += [ref[j], ref[NZL + j], swapped[at], swapped[at + NZL]]
        total += jnp.dot(
            jnp.concatenate(left, axis=1),
            jnp.concatenate(right, axis=0),
            preferred_element_type=F32,
        )
    o_ref[...] = (total * scale).astype(BF)


def project(near, far, ring, swapped, scale):
    rows = near[0].shape[0]
    cols = ring[0].shape[-1]
    full = pl.BlockSpec(memory_space=pltpu.VMEM)
    operands = [*near, *far, *ring, swapped]
    return pl.pallas_call(
        lambda *refs: project_body(*refs, scale=scale),
        out_shape=jax.ShapeDtypeStruct((rows, cols), BF),
        in_specs=[full] * len(operands),
        out_specs=full,
        cost_estimate=pl.CostEstimate(
            flops=2 * rows * 4096 * cols,
            bytes_accessed=2 * (rows * 4096 + cols * 4096 + rows * cols),
            transcendentals=0,
        ),
        compiler_params=pltpu.CompilerParams(vmem_limit_bytes=20 * MIB),
        name="project",
    )(*operands)


def ring_y(block):
    out = [block]
    for _ in range(4):
        out.append(hop(out[-1], dy=1, by_core=True))
    return out


def ring_x(block):
    one = hop(block, dx=1, by_core=True)
    three = hop(block, dx=3, by_core=True)
    two = hop(one, dx=1, by_core=True)
    return [block, one, two, three]


def join_body(*refs):
    *parts, o_ref = refs
    n = parts[0].shape[0]
    for i, part in enumerate(parts):
        o_ref[i * n : (i + 1) * n] = part[...]


def joined_blocks(blocks):
    full = pl.BlockSpec(memory_space=pltpu.VMEM)
    shape = (len(blocks) * blocks[0].shape[0],) + blocks[0].shape[1:]
    return pl.pallas_call(
        join_body,
        out_shape=jax.ShapeDtypeStruct(shape, BF),
        in_specs=[full] * len(blocks),
        out_specs=full,
        cost_estimate=pl.CostEstimate(flops=0, bytes_accessed=4 * 2**20, transcendentals=0),
        compiler_params=pltpu.CompilerParams(vmem_limit_bytes=8 * MIB),
        name="join",
    )(*blocks)


def gather_zcore(w):
    w = w[None]
    line = joined_blocks([w] + [hop(w, flip=j) for j in (1, 2, 3)])
    chips = [
        [z * 2 * NY + 2 * y + core for core in range(2)] for z in range(NZL) for y in range(NY)
    ]
    w = lax.all_gather(line, "ctx", axis=0, tiled=False, axis_index_groups=chips)
    return w.reshape((2 * NZL,) + w.shape[2:])


TILE = 256
REACH = 5 * TILE


NT = (((1,), (1,)), ((), ()))


def tile_at(i, h):
    col0 = pl.multiple_of(h * HEAD_SIZE, HEAD_SIZE)
    return slice(i * TILE, (i + 1) * TILE), pl.ds(col0, HEAD_SIZE)


def first_allowed(len_ref, rows, row):
    docs = len_ref.shape[1]
    lead = lax.axis_index("ctx").astype(jnp.int32) * rows
    i0 = lax.broadcasted_iota(jnp.int32, (docs, docs), 0)
    i1 = lax.broadcasted_iota(jnp.int32, (docs, docs), 1)
    starts = jnp.sum(jnp.where(i1 < i0, len_ref[...], 0), axis=1, keepdims=True)
    begin = jnp.max(jnp.where(starts <= lead + row, starts, 0), axis=0, keepdims=True)
    return jnp.maximum(begin - lead + WINDOW, row + 1)


def block_scores(keys, q, first, low, high):
    s = lax.dot_general(keys, q, NT, preferred_element_type=F32)
    key = first + lax.broadcasted_iota(jnp.int32, (TILE, 1), 0)
    return jnp.where((key >= low) & (key <= high), s, -1e30)


def span(k):
    return slice(k * TILE, (k + 1) * TILE)


def near_body(len_ref, q_ref, own, e1, g_ref, e_ref, d_ref, stat_ref):
    rows = q_ref.shape[0]
    for i in range(2):

        @pl.loop(0, 2)
        def _(h):
            step = 2 * h + i
            q, g = q_ref[tile_at(i, h)], g_ref[tile_at(i, h)]
            row = i * TILE + lax.broadcasted_iota(jnp.int32, (1, TILE), 1)
            low = first_allowed(len_ref, rows, row) - rows
            high = row + (WINDOW - rows)
            peak = jnp.full((1, TILE), -1e30, F32)
            for k in range(3 + i):
                keys = (e1 if k < 2 else own)[span(k % 2), :HEAD_SIZE]
                s = block_scores(keys, q, k * TILE, low, high)
                e_ref[step, span(k)] = s
                peak = jnp.maximum(peak, jnp.max(s, axis=0, keepdims=True))
            total = jnp.zeros((1, TILE), F32)
            weighted = jnp.zeros((1, TILE), F32)
            for k in range(3 + i):
                values = (e1 if k < 2 else own)[span(k % 2), HEAD_SIZE:]
                d = lax.dot_general(values, g, NT, preferred_element_type=F32)
                e = jnp.exp(e_ref[step, span(k)] - peak)
                e_ref[step, span(k)] = e
                d_ref[step, span(k)] = d
                total += jnp.sum(e, axis=0, keepdims=True)
                weighted += jnp.sum(e * d, axis=0, keepdims=True)
            stat_ref[step, 0:1] = peak
            stat_ref[step, 1:2] = total
            stat_ref[step, 2:3] = weighted


def far_body(len_ref, q_ref, e2, g_ref, e_ref, d_ref, stat_ref, p_ref, dk0, dk1, dk2, s_ref, t_ref, acc):
    rows = q_ref.shape[0]
    acc[...] = jnp.zeros_like(acc)
    for i in range(2):

        @pl.loop(0, 2)
        def _(h):
            step = 2 * h + i
            q, g = q_ref[tile_at(i, h)], g_ref[tile_at(i, h)]
            row = i * TILE + lax.broadcasted_iota(jnp.int32, (1, TILE), 1)
            low = first_allowed(len_ref, rows, row)
            near_peak = stat_ref[step, 0:1]
            peak = near_peak
            for k in range(i, 2):
                s = block_scores(e2[span(k), :HEAD_SIZE], q, k * TILE, low, 2 * rows)
                s_ref[span(k)] = s
                peak = jnp.maximum(peak, jnp.max(s, axis=0, keepdims=True))
            shrink = jnp.exp(near_peak - peak)
            total = stat_ref[step, 1:2] * shrink
            weighted = stat_ref[step, 2:3] * shrink
            for k in range(i, 2):
                d = lax.dot_general(e2[span(k), HEAD_SIZE:], g, NT, preferred_element_type=F32)
                e = jnp.exp(s_ref[span(k)] - peak)
                s_ref[span(k)] = e
                t_ref[span(k)] = d
                total += jnp.sum(e, axis=0, keepdims=True)
                weighted += jnp.sum(e * d, axis=0, keepdims=True)
            inverse = 1.0 / total
            delta = weighted * inverse
            near_scale = shrink * inverse
            for k in range(i, i + 5):
                if k < 2:
                    p, d = s_ref[span(k)] * inverse, t_ref[span(k)]
                else:
                    p, d = e_ref[step, span(k - 2)] * near_scale, d_ref[step, span(k - 2)]
                p_ref[step, span(k - i)] = p.astype(BF)
                ds = (p * (d - delta)).astype(BF)
                acc[span(k)] += jnp.dot(ds, q, preferred_element_type=F32)

    dk2[...] = acc[0:rows].astype(BF)
    dk1[...] = acc[rows : 2 * rows].astype(BF)
    dk0[...] = acc[2 * rows : 3 * rows]


def values_body(p_ref, own, e1, e2, o_ref):
    tn = (((0,), (0,)), ((), ()))
    for i in range(2):
        value = jnp.concatenate(
            [e2[i * TILE :, HEAD_SIZE:], e1[:, HEAD_SIZE:], own[: (i + 1) * TILE, HEAD_SIZE:]], axis=0
        )
        for h in range(2):
            a = lax.dot_general(p_ref[2 * h + i], value, tn, preferred_element_type=F32)
            o_ref[i * TILE : (i + 1) * TILE, h * HEAD_SIZE : (h + 1) * HEAD_SIZE] = a.astype(BF)


def attend(lens, query, own, e1, e2, grad):
    rows = query.shape[0]
    full = pl.BlockSpec(memory_space=pltpu.VMEM)
    shape = jax.ShapeDtypeStruct
    pairs = 4 * TILE * REACH
    e, d, stat = pl.pallas_call(
        near_body,
        out_shape=(
            shape((4, 2 * rows, TILE), F32),
            shape((4, 2 * rows, TILE), F32),
            shape((4, 8, TILE), F32),
        ),
        in_specs=[full] * 5,
        out_specs=(full,) * 3,
        cost_estimate=pl.CostEstimate(
            flops=3 * pairs * HEAD_SIZE, bytes_accessed=5 * rows * 1024 + 8 * pairs, transcendentals=pairs
        ),
        compiler_params=pltpu.CompilerParams(vmem_limit_bytes=16 * MIB),
        name="near_scores",
    )(lens, query, own, e1, grad)
    p, dk0, dk1, dk2 = pl.pallas_call(
        far_body,
        out_shape=(
            shape((4, REACH, TILE), BF),
            shape((rows, HEAD_SIZE), F32),
            shape((rows, HEAD_SIZE), BF),
            shape((rows, HEAD_SIZE), BF),
        ),
        in_specs=[full] * 7,
        out_specs=(full,) * 4,
        scratch_shapes=[
            pltpu.VMEM((rows, TILE), F32),
            pltpu.VMEM((rows, TILE), F32),
            pltpu.VMEM((3 * rows, HEAD_SIZE), F32),
        ],
        cost_estimate=pl.CostEstimate(
            flops=3 * pairs * HEAD_SIZE, bytes_accessed=5 * rows * 1024 + 10 * pairs, transcendentals=pairs
        ),
        compiler_params=pltpu.CompilerParams(vmem_limit_bytes=20 * MIB),
        name="far_scores",
    )(lens, query, e2, grad, e, d, stat)
    out = pl.pallas_call(
        values_body,
        out_shape=shape((rows, 2 * HEAD_SIZE), BF),
        in_specs=[full] * 4,
        out_specs=full,
        cost_estimate=pl.CostEstimate(
            flops=2 * pairs * HEAD_SIZE, bytes_accessed=4 * rows * 1024 + 2 * pairs, transcendentals=0
        ),
        compiler_params=pltpu.CompilerParams(vmem_limit_bytes=14 * MIB),
        name="values",
    )(p, own, e1, e2)
    return out, dk0, dk1, dk2


def local(tokens, w_query, key_matrix, value_matrix, d_attended, doc_lengths):
    feature = jnp.arange(tokens.shape[1], dtype=jnp.int32)
    target = feature // ROWS * PAD + feature % ROWS
    spread = (target[:, None] == jnp.arange(8 * PAD, dtype=jnp.int32)[None, :]).astype(BF)
    own = jnp.dot(tokens, spread, preferred_element_type=F32).astype(BF)

    partner = hop(own, dz=NZL)
    near = ring_x(own)
    far = ring_x(partner)

    w = gather_zcore(jnp.concatenate([key_matrix, value_matrix, w_query], axis=1))
    w = jnp.pad(w, ((0, 0), (0, PAD - ROWS), (0, 0)))
    kv_cols = 2 * HEAD_SIZE
    kv = ring_y(w[..., :kv_cols])
    kv_a = hop(joined_blocks(kv[1:4]), swap=1)
    qs = ring_y(w[..., kv_cols:])
    q_a = hop(joined_blocks(qs[1:4]), swap=1)

    joined = project(near, far, kv, kv_a, 1.0)
    query = project(near, far, qs, q_a, 0.0625)

    e2 = along_ctx(joined, 2)
    e1 = along_ctx(joined, 1)
    attended, dk0, dk1, dk2 = attend(
        doc_lengths.reshape(1, -1), query, joined, e1, e2, d_attended
    )
    key_total = dk0 + along_ctx(dk2, -2).astype(F32) + along_ctx(dk1, -1).astype(F32)
    return (attended, key_total.astype(BF))


def solution(mesh):
    return jax.shard_map(
        local,
        mesh=mesh,
        in_specs=(
            P("ctx", "head"),
            P("ctx", "head"),
            P("ctx", "head"),
            P("ctx", "head"),
            P("ctx", "head"),
            P(),
        ),
        out_specs=(P("ctx", "head"), P("ctx", "head")),
        check_vma=False,
    )
```

profile of v0, /device:TPU:199, one launch (start us, length us, event | category | flops | bytes accessed | tf_op | source)
XLA Modules:
  0.0 152.7 jit_solution(2518264522085084868)
XLA Ops:
  3.5 2.5 %collective-permute-start.8 = (bf16[1,60,1024]{2,1,0:T(8,128)(2,1)S(1)}, bf16[1,60,1024]{2,1,0:T(8,128)(2,1)S(1)}, u32[]{:S(2)}, u32[]{:S(2)}) collective-permute-start(bf16[1,60,1024]{2,1,0:T(8,128)(2,1)S(1)} %maximum_bitcast_fusion.refs_0_), channel_id=1, source_target_pairs={{0,256},{8,264},{128,384},{136,392},{256,0},{264,8},{384,128},{392... | collective-permute-start | bytes 368648 | tf_op jit(solution)/shard_map/ppermute | solution.py:41
  5.9 4.9 %collective-permute-start.7 = (bf16[1,60,1024]{2,1,0:T(8,128)(2,1)S(1)}, bf16[1,60,1024]{2,1,0:T(8,128)(2,1)S(1)}, u32[]{:S(2)}, u32[]{:S(2)}) collective-permute-start(bf16[1,60,1024]{2,1,0:T(8,128)(2,1)S(1)} %maximum_bitcast_fusion.refs_0_), channel_id=1, source_target_pairs={{0,128},{8,136},{128,0},{136,8},{256,384},{264,392},{384,256},{392... | collective-permute-start | bytes 368648 | tf_op jit(solution)/shard_map/ppermute | solution.py:41
  10.9 5.7 %collective-permute-done.8.refs_2_ = bf16[1,60,1024]{2,1,0:T(8,128)(2,1)S(1)} collective-permute-done((bf16[1,60,1024]{2,1,0:T(8,128)(2,1)S(1)}, bf16[1,60,1024]{2,1,0:T(8,128)(2,1)S(1)}, u32[]{:S(2)}, u32[]{:S(2)}) %collective-permute-start.8) | collective-permute-done | bytes 122912 | tf_op jit(solution)/shard_map/ppermute | solution.py:41
  16.7 3.6 %all-gather = bf16[8,60,1024]{2,1,0:T(8,128)(2,1)S(1)} all-gather(bf16[4,60,1024]{2,1,0:T(8,128)(2,1)S(1)} %join.3), channel_id=2, replica_groups={{0,8},{16,24},{32,40},{48,56},{64,72},{80,88},{96,104},{112,120},{128,1..., dimensions={0}, use_global_device_ids=true | all-gather | bytes 1474560 | tf_op jit(solution)/shard_map/all_gather | solution.py:142
  20.4 5.1 %collective-permute-start.15 = (bf16[8,64,512]{2,1,0:T(8,128)(2,1)S(1)}, bf16[8,64,512]{2,1,0:T(8,128)(2,1)S(1)}, u32[]{:S(2)}, u32[]{:S(2)}) collective-permute-start(bf16[8,64,512]{2,1,0:T(8,128)(2,1)S(1)} %get-tuple-element.16.refs_8_), channel_id=1, source_target_pairs={{0,16},{8,120},{128,144},{136,248},{256,272},{264,376},{384,400},{... | collective-permute-start | bytes 1572872 | tf_op jit(solution)/shard_map/ppermute | solution.py:41
  25.5 3.0 %collective-permute-start.10 = (bf16[8,64,512]{2,1,0:T(8,128)(2,1)S(1)}, bf16[8,64,512]{2,1,0:T(8,128)(2,1)S(1)}, u32[]{:S(2)}, u32[]{:S(2)}) collective-permute-start(bf16[8,64,512]{2,1,0:T(8,128)(2,1)S(1)} %get-tuple-element.17.refs_8_), channel_id=1, source_target_pairs={{0,16},{8,120},{128,144},{136,248},{256,272},{264,376},{384,400},{... | collective-permute-start | bytes 1572872 | tf_op jit(solution)/shard_map/ppermute | solution.py:41
  28.5 3.1 %collective-permute-done.15.refs_0_.refs_9_ = bf16[8,64,512]{2,1,0:T(8,128)(2,1)S(1)} collective-permute-done((bf16[8,64,512]{2,1,0:T(8,128)(2,1)S(1)}, bf16[8,64,512]{2,1,0:T(8,128)(2,1)S(1)}, u32[]{:S(2)}, u32[]{:S(2)}) %collective-permute-start.15) | collective-permute-done | bytes 524320 | tf_op jit(solution)/shard_map/ppermute | solution.py:41
  31.7 5.0 %collective-permute-start.16 = (bf16[8,64,512]{2,1,0:T(8,128)(2,1)S(1)}, bf16[8,64,512]{2,1,0:T(8,128)(2,1)S(1)}, u32[]{:S(2)}, u32[]{:S(2)}) collective-permute-start(bf16[8,64,512]{2,1,0:T(8,128)(2,1)S(1)} %collective-permute-done.15.refs_0_.refs_9_), channel_id=1, source_target_pairs={{0,16},{8,120},{128,144},{136,248},{256,272},{264,376},{384,400},{... | collective-permute-start | bytes 1572872 | tf_op jit(solution)/shard_map/ppermute | solution.py:41
  37.3 5.0 %collective-permute-start.11 = (bf16[8,64,512]{2,1,0:T(8,128)(2,1)S(1)}, bf16[8,64,512]{2,1,0:T(8,128)(2,1)S(1)}, u32[]{:S(2)}, u32[]{:S(2)}) collective-permute-start(bf16[8,64,512]{2,1,0:T(8,128)(2,1)S(1)} %collective-permute-done.10.refs_0_.refs_9_), channel_id=1, source_target_pairs={{0,16},{8,120},{128,144},{136,248},{256,272},{264,376},{384,400},{... | collective-permute-start | bytes 1572872 | tf_op jit(solution)/shard_map/ppermute | solution.py:41
  42.9 5.0 %collective-permute-start.17 = (bf16[8,64,512]{2,1,0:T(8,128)(2,1)S(1)}, bf16[8,64,512]{2,1,0:T(8,128)(2,1)S(1)}, u32[]{:S(2)}, u32[]{:S(2)}) collective-permute-start(bf16[8,64,512]{2,1,0:T(8,128)(2,1)S(1)} %collective-permute-done.16.refs_1_.refs_10_), channel_id=1, source_target_pairs={{0,16},{8,120},{128,144},{136,248},{256,272},{264,376},{384,400},{... | collective-permute-start | bytes 1572872 | tf_op jit(solution)/shard_map/ppermute | solution.py:41
  48.5 7.9 %collective-permute-start.3 = (bf16[512,512]{1,0:T(8,128)(2,1)S(1)}, bf16[512,512]{1,0:T(8,128)(2,1)S(1)}, u32[]{:S(2)}, u32[]{:S(2)}) collective-permute-start(bf16[512,512]{1,0:T(8,128)(2,1)S(1)} %fusion.refs_0_), channel_id=1, source_target_pairs={{0,1},{8,9},{128,129},{136,137},{256,257},{264,265},{384,385},{392... | collective-permute-start | bytes 1572872 | tf_op jit(solution)/shard_map/ppermute | solution.py:41
  60.8 2.9 %collective-permute-start.19 = (bf16[24,64,512]{2,1,0:T(8,128)(2,1)S(1)}, bf16[24,64,512]{2,1,0:T(8,128)(2,1)S(1)}, u32[]{:S(2)}, u32[]{:S(2)}) collective-permute-start(bf16[24,64,512]{2,1,0:T(8,128)(2,1)S(1)} %join.5), channel_id=1, source_target_pairs={{0,8},{8,0},{128,136},{136,128},{256,264},{264,256},{384,392},{392... | collective-permute-start | bytes 4718600 | tf_op jit(solution)/shard_map/ppermute | solution.py:41
  65.9 14.0 %collective-permute-done.3.refs_4_ = bf16[512,512]{1,0:T(8,128)(2,1)S(1)} collective-permute-done((bf16[512,512]{1,0:T(8,128)(2,1)S(1)}, bf16[512,512]{1,0:T(8,128)(2,1)S(1)}, u32[]{:S(2)}, u32[]{:S(2)}) %collective-permute-start.3) | collective-permute-done | bytes 524320 | tf_op jit(solution)/shard_map/ppermute | solution.py:41
  79.9 2.5 %collective-permute-start.4 = (bf16[512,512]{1,0:T(8,128)(2,1)S(1)}, bf16[512,512]{1,0:T(8,128)(2,1)S(1)}, u32[]{:S(2)}, u32[]{:S(2)}) collective-permute-start(bf16[512,512]{1,0:T(8,128)(2,1)S(1)} %collective-permute-done.3.refs_4_), channel_id=1, source_target_pairs={{0,2},{8,14},{128,130},{136,142},{256,258},{264,270},{384,386},{39... | collective-permute-start | bytes 1572872 | tf_op jit(solution)/shard_map/ppermute | solution.py:41
  82.4 4.0 %collective-permute-start.6 = (bf16[512,512]{1,0:T(8,128)(2,1)S(1)}, bf16[512,512]{1,0:T(8,128)(2,1)S(1)}, u32[]{:S(2)}, u32[]{:S(2)}) collective-permute-start(bf16[512,512]{1,0:T(8,128)(2,1)S(1)} %collective-permute-done.3.refs_4_), channel_id=1, source_target_pairs={{0,6},{8,10},{128,134},{136,138},{256,262},{264,266},{384,390},{39... | collective-permute-start | bytes 1572872 | tf_op jit(solution)/shard_map/ppermute | solution.py:41
  90.7 2.9 %collective-permute-done.4.refs_5_ = bf16[512,512]{1,0:T(8,128)(2,1)S(1)} collective-permute-done((bf16[512,512]{1,0:T(8,128)(2,1)S(1)}, bf16[512,512]{1,0:T(8,128)(2,1)S(1)}, u32[]{:S(2)}, u32[]{:S(2)}) %collective-permute-start.4) | collective-permute-done | bytes 524320 | tf_op jit(solution)/shard_map/ppermute | solution.py:41
  95.6 2.7 %collective-permute-done.6.refs_7_ = bf16[512,512]{1,0:T(8,128)(2,1)S(1)} collective-permute-done((bf16[512,512]{1,0:T(8,128)(2,1)S(1)}, bf16[512,512]{1,0:T(8,128)(2,1)S(1)}, u32[]{:S(2)}, u32[]{:S(2)}) %collective-permute-start.6) | collective-permute-done | bytes 524320 | tf_op jit(solution)/shard_map/ppermute | solution.py:41
  104.2 4.0 %collective-permute-done.5.refs_6_ = bf16[512,512]{1,0:T(8,128)(2,1)S(1)} collective-permute-done((bf16[512,512]{1,0:T(8,128)(2,1)S(1)}, bf16[512,512]{1,0:T(8,128)(2,1)S(1)}, u32[]{:S(2)}, u32[]{:S(2)}) %collective-permute-start.5) | collective-permute-done | bytes 524320 | tf_op jit(solution)/shard_map/ppermute | solution.py:41
  110.8 4.3 %collective-permute-start.21 = (bf16[512,512]{1,0:T(8,128)(2,1)S(1)}, bf16[512,512]{1,0:T(8,128)(2,1)S(1)}, u32[]{:S(2)}, u32[]{:S(2)}) collective-permute-start(bf16[512,512]{1,0:T(8,128)(2,1)S(1)} %project.3.own), channel_id=1, source_target_pairs={{0,8},{8,16},{16,24},{24,32},{32,40},{40,48},{48,56},{56,64},{64,7... | collective-permute-start | bytes 1572872 | tf_op jit(solution)/shard_map/ppermute | solution.py:47
  117.1 2.4 %project.2.q_ref = bf16[512,512]{1,0:T(8,128)(2,1)S(1)} custom-call(bf16[512,512]{1,0:T(8,128)(2,1)S(1)} %fusion.refs_0_, bf16[512,512]{1,0:T(8,128)(2,1)S(1)} %collective-permute-done.refs_1_, bf16[512,512]{1,0:T(8,128)(2,1)S(1)} %collective-permute-done.1.refs_2_, bf16[512,512]{1,0:T(8,128)(2,1)S(1)} %collective-permute-done.2.refs_3_, ...), custom_call_target="tpu_custom_call" | custom-call | flops 2147483648 | bytes 8912896 | tf_op jit(solution)/shard_map/project/pallas_call | solution.py:86
  119.5 3.6 %collective-permute-done.21.e1 = bf16[512,512]{1,0:T(8,128)(2,1)S(1)} collective-permute-done((bf16[512,512]{1,0:T(8,128)(2,1)S(1)}, bf16[512,512]{1,0:T(8,128)(2,1)S(1)}, u32[]{:S(2)}, u32[]{:S(2)}) %collective-permute-start.21) | collective-permute-done | bytes 524320 | tf_op jit(solution)/shard_map/ppermute | solution.py:47
  125.4 12.5 %collective-permute-done.20.e2 = bf16[512,512]{1,0:T(8,128)(2,1)S(1)} collective-permute-done((bf16[512,512]{1,0:T(8,128)(2,1)S(1)}, bf16[512,512]{1,0:T(8,128)(2,1)S(1)}, u32[]{:S(2)}, u32[]{:S(2)}) %collective-permute-start.20) | collective-permute-done | bytes 524320 | tf_op jit(solution)/shard_map/ppermute | solution.py:47
  138.0 3.2 %far_scores.1 = (bf16[4,1280,256]{2,1,0:T(8,128)(2,1)S(1)}, f32[512,256]{1,0:T(8,128)S(1)}, bf16[512,256]{1,0:T(8,128)(2,1)S(1)}, bf16[512,256]{1,0:T(8,128)(2,1)S(1)}) custom-call(s32[1,32]{1,0:T(1,128)S(1)} %bitcast.7, bf16[512,512]{1,0:T(8,128)(2,1)S(1)} %project.2.q_ref, bf16[512,512]{1,0:T(8,128)(2,1)S(1)} %collective-permute-done.20.e2, ...), custom_call_target="tpu_custom_call" | custom-call | flops 1006632960 | bytes 15728640 | tf_op jit(solution)/shard_map/far_scores/pallas_call | solution.py:285
  146.7 3.5 %collective-permute-done.22 = bf16[512,256]{1,0:T(8,128)(2,1)S(1)} collective-permute-done((bf16[512,256]{1,0:T(8,128)(2,1)S(1)}, bf16[512,256]{1,0:T(8,128)(2,1)S(1)}, u32[]{:S(2)}, u32[]{:S(2)}) %collective-permute-start.22) | collective-permute-done | bytes 262176 | tf_op jit(solution)/shard_map/ppermute | solution.py:47
  (44 shorter events, 38.3 us)
Async XLA Ops:
  1.6 9.3 %collective-permute-start.9 = (bf16[1,60,1024]{2,1,0:T(8,128)(2,1)S(1)}, bf16[1,60,1024]{2,1,0:T(8,128)(2,1)S(1)}, u32[]{:S(2)}, u32[]{:S(2)}) collective-permute-start(bf16[1,60,1024]{2,1,0:T(8,128)(2,1)S(1)} %maximum_bitcast_fusion.refs_0_), channel_id=1, source_target_pairs={{0,384},{8,392},{128,256},{136,264},{256,128},{264,136},{384,0},{3... | collective-permute-start | bytes 368648 | tf_op jit(solution)/shard_map/ppermute | solution.py:41
  3.5 13.0 %collective-permute-start.8 = (bf16[1,60,1024]{2,1,0:T(8,128)(2,1)S(1)}, bf16[1,60,1024]{2,1,0:T(8,128)(2,1)S(1)}, u32[]{:S(2)}, u32[]{:S(2)}) collective-permute-start(bf16[1,60,1024]{2,1,0:T(8,128)(2,1)S(1)} %maximum_bitcast_fusion.refs_0_), channel_id=1, source_target_pairs={{0,256},{8,264},{128,384},{136,392},{256,0},{264,8},{384,128},{392... | collective-permute-start | bytes 368648 | tf_op jit(solution)/shard_map/ppermute | solution.py:41
  5.9 10.7 %collective-permute-start.7 = (bf16[1,60,1024]{2,1,0:T(8,128)(2,1)S(1)}, bf16[1,60,1024]{2,1,0:T(8,128)(2,1)S(1)}, u32[]{:S(2)}, u32[]{:S(2)}) collective-permute-start(bf16[1,60,1024]{2,1,0:T(8,128)(2,1)S(1)} %maximum_bitcast_fusion.refs_0_), channel_id=1, source_target_pairs={{0,128},{8,136},{128,0},{136,8},{256,384},{264,392},{384,256},{392... | collective-permute-start | bytes 368648 | tf_op jit(solution)/shard_map/ppermute | solution.py:41
  20.4 11.2 %collective-permute-start.15 = (bf16[8,64,512]{2,1,0:T(8,128)(2,1)S(1)}, bf16[8,64,512]{2,1,0:T(8,128)(2,1)S(1)}, u32[]{:S(2)}, u32[]{:S(2)}) collective-permute-start(bf16[8,64,512]{2,1,0:T(8,128)(2,1)S(1)} %get-tuple-element.16.refs_8_), channel_id=1, source_target_pairs={{0,16},{8,120},{128,144},{136,248},{256,272},{264,376},{384,400},{... | collective-permute-start | bytes 1572872 | tf_op jit(solution)/shard_map/ppermute | solution.py:41
  25.5 11.7 %collective-permute-start.10 = (bf16[8,64,512]{2,1,0:T(8,128)(2,1)S(1)}, bf16[8,64,512]{2,1,0:T(8,128)(2,1)S(1)}, u32[]{:S(2)}, u32[]{:S(2)}) collective-permute-start(bf16[8,64,512]{2,1,0:T(8,128)(2,1)S(1)} %get-tuple-element.17.refs_8_), channel_id=1, source_target_pairs={{0,16},{8,120},{128,144},{136,248},{256,272},{264,376},{384,400},{... | collective-permute-start | bytes 1572872 | tf_op jit(solution)/shard_map/ppermute | solution.py:41
  31.7 11.2 %collective-permute-start.16 = (bf16[8,64,512]{2,1,0:T(8,128)(2,1)S(1)}, bf16[8,64,512]{2,1,0:T(8,128)(2,1)S(1)}, u32[]{:S(2)}, u32[]{:S(2)}) collective-permute-start(bf16[8,64,512]{2,1,0:T(8,128)(2,1)S(1)} %collective-permute-done.15.refs_0_.refs_9_), channel_id=1, source_target_pairs={{0,16},{8,120},{128,144},{136,248},{256,272},{264,376},{384,400},{... | collective-permute-start | bytes 1572872 | tf_op jit(solution)/shard_map/ppermute | solution.py:41
  37.3 19.2 %collective-permute-start.11 = (bf16[8,64,512]{2,1,0:T(8,128)(2,1)S(1)}, bf16[8,64,512]{2,1,0:T(8,128)(2,1)S(1)}, u32[]{:S(2)}, u32[]{:S(2)}) collective-permute-start(bf16[8,64,512]{2,1,0:T(8,128)(2,1)S(1)} %collective-permute-done.10.refs_0_.refs_9_), channel_id=1, source_target_pairs={{0,16},{8,120},{128,144},{136,248},{256,272},{264,376},{384,400},{... | collective-permute-start | bytes 1572872 | tf_op jit(solution)/shard_map/ppermute | solution.py:41
  42.9 17.8 %collective-permute-start.17 = (bf16[8,64,512]{2,1,0:T(8,128)(2,1)S(1)}, bf16[8,64,512]{2,1,0:T(8,128)(2,1)S(1)}, u32[]{:S(2)}, u32[]{:S(2)}) collective-permute-start(bf16[8,64,512]{2,1,0:T(8,128)(2,1)S(1)} %collective-permute-done.16.refs_1_.refs_10_), channel_id=1, source_target_pairs={{0,16},{8,120},{128,144},{136,248},{256,272},{264,376},{384,400},{... | collective-permute-start | bytes 1572872 | tf_op jit(solution)/shard_map/ppermute | solution.py:41
  48.5 31.4 %collective-permute-start.3 = (bf16[512,512]{1,0:T(8,128)(2,1)S(1)}, bf16[512,512]{1,0:T(8,128)(2,1)S(1)}, u32[]{:S(2)}, u32[]{:S(2)}) collective-permute-start(bf16[512,512]{1,0:T(8,128)(2,1)S(1)} %fusion.refs_0_), channel_id=1, source_target_pairs={{0,1},{8,9},{128,129},{136,137},{256,257},{264,265},{384,385},{392... | collective-permute-start | bytes 1572872 | tf_op jit(solution)/shard_map/ppermute | solution.py:41
  56.5 25.9 %collective-permute-start.12 = (bf16[8,64,512]{2,1,0:T(8,128)(2,1)S(1)}, bf16[8,64,512]{2,1,0:T(8,128)(2,1)S(1)}, u32[]{:S(2)}, u32[]{:S(2)}) collective-permute-start(bf16[8,64,512]{2,1,0:T(8,128)(2,1)S(1)} %collective-permute-done.11.refs_1_.refs_10_), channel_id=1, source_target_pairs={{0,16},{8,120},{128,144},{136,248},{256,272},{264,376},{384,400},{... | collective-permute-start | bytes 1572872 | tf_op jit(solution)/shard_map/ppermute | solution.py:41
  58.5 28.0 %collective-permute-start.2 = (bf16[512,512]{1,0:T(8,128)(2,1)S(1)}, bf16[512,512]{1,0:T(8,128)(2,1)S(1)}, u32[]{:S(2)}, u32[]{:S(2)}) collective-permute-start(bf16[512,512]{1,0:T(8,128)(2,1)S(1)} %fusion.refs_0_), channel_id=1, source_target_pairs={{0,6},{8,10},{128,134},{136,138},{256,262},{264,266},{384,390},{39... | collective-permute-start | bytes 1572872 | tf_op jit(solution)/shard_map/ppermute | solution.py:41
  60.8 47.7 %collective-permute-start.19 = (bf16[24,64,512]{2,1,0:T(8,128)(2,1)S(1)}, bf16[24,64,512]{2,1,0:T(8,128)(2,1)S(1)}, u32[]{:S(2)}, u32[]{:S(2)}) collective-permute-start(bf16[24,64,512]{2,1,0:T(8,128)(2,1)S(1)} %join.5), channel_id=1, source_target_pairs={{0,8},{8,0},{128,136},{136,128},{256,264},{264,256},{384,392},{392... | collective-permute-start | bytes 4718600 | tf_op jit(solution)/shard_map/ppermute | solution.py:41
  63.7 24.7 %collective-permute-start = (bf16[512,512]{1,0:T(8,128)(2,1)S(1)}, bf16[512,512]{1,0:T(8,128)(2,1)S(1)}, u32[]{:S(2)}, u32[]{:S(2)}) collective-permute-start(bf16[512,512]{1,0:T(8,128)(2,1)S(1)} %fusion.refs_0_), channel_id=1, source_target_pairs={{0,2},{8,14},{128,130},{136,142},{256,258},{264,270},{384,386},{39... | collective-permute-start | bytes 1572872 | tf_op jit(solution)/shard_map/ppermute | solution.py:41
  79.9 13.7 %collective-permute-start.4 = (bf16[512,512]{1,0:T(8,128)(2,1)S(1)}, bf16[512,512]{1,0:T(8,128)(2,1)S(1)}, u32[]{:S(2)}, u32[]{:S(2)}) collective-permute-start(bf16[512,512]{1,0:T(8,128)(2,1)S(1)} %collective-permute-done.3.refs_4_), channel_id=1, source_target_pairs={{0,2},{8,14},{128,130},{136,142},{256,258},{264,270},{384,386},{39... | collective-permute-start | bytes 1572872 | tf_op jit(solution)/shard_map/ppermute | solution.py:41
  82.4 15.8 %collective-permute-start.6 = (bf16[512,512]{1,0:T(8,128)(2,1)S(1)}, bf16[512,512]{1,0:T(8,128)(2,1)S(1)}, u32[]{:S(2)}, u32[]{:S(2)}) collective-permute-start(bf16[512,512]{1,0:T(8,128)(2,1)S(1)} %collective-permute-done.3.refs_4_), channel_id=1, source_target_pairs={{0,6},{8,10},{128,134},{136,138},{256,262},{264,266},{384,390},{39... | collective-permute-start | bytes 1572872 | tf_op jit(solution)/shard_map/ppermute | solution.py:41
  86.5 30.5 %collective-permute-start.14 = (bf16[24,64,512]{2,1,0:T(8,128)(2,1)S(1)}, bf16[24,64,512]{2,1,0:T(8,128)(2,1)S(1)}, u32[]{:S(2)}, u32[]{:S(2)}) collective-permute-start(bf16[24,64,512]{2,1,0:T(8,128)(2,1)S(1)} %join.4), channel_id=1, source_target_pairs={{0,8},{8,0},{128,136},{136,128},{256,264},{264,256},{384,392},{392... | collective-permute-start | bytes 4718600 | tf_op jit(solution)/shard_map/ppermute | solution.py:41
  88.5 13.8 %collective-permute-start.1 = (bf16[512,512]{1,0:T(8,128)(2,1)S(1)}, bf16[512,512]{1,0:T(8,128)(2,1)S(1)}, u32[]{:S(2)}, u32[]{:S(2)}) collective-permute-start(bf16[512,512]{1,0:T(8,128)(2,1)S(1)} %collective-permute-done.refs_1_), channel_id=1, source_target_pairs={{0,2},{8,14},{128,130},{136,142},{256,258},{264,270},{384,386},{39... | collective-permute-start | bytes 1572872 | tf_op jit(solution)/shard_map/ppermute | solution.py:41
  93.6 14.5 %collective-permute-start.5 = (bf16[512,512]{1,0:T(8,128)(2,1)S(1)}, bf16[512,512]{1,0:T(8,128)(2,1)S(1)}, u32[]{:S(2)}, u32[]{:S(2)}) collective-permute-start(bf16[512,512]{1,0:T(8,128)(2,1)S(1)} %collective-permute-done.4.refs_5_), channel_id=1, source_target_pairs={{0,2},{8,14},{128,130},{136,142},{256,258},{264,270},{384,386},{39... | collective-permute-start | bytes 1572872 | tf_op jit(solution)/shard_map/ppermute | solution.py:41
  98.2 10.2 %collective-permute-start.18 = (bf16[8,64,512]{2,1,0:T(8,128)(2,1)S(1)}, bf16[8,64,512]{2,1,0:T(8,128)(2,1)S(1)}, u32[]{:S(2)}, u32[]{:S(2)}) collective-permute-start(bf16[8,64,512]{2,1,0:T(8,128)(2,1)S(1)} %collective-permute-done.17.refs_2_.refs_11_), channel_id=1, source_target_pairs={{0,16},{8,120},{128,144},{136,248},{256,272},{264,376},{384,400},{... | collective-permute-start | bytes 1572872 | tf_op jit(solution)/shard_map/ppermute | solution.py:41
  102.3 14.8 %collective-permute-start.13 = (bf16[8,64,512]{2,1,0:T(8,128)(2,1)S(1)}, bf16[8,64,512]{2,1,0:T(8,128)(2,1)S(1)}, u32[]{:S(2)}, u32[]{:S(2)}) collective-permute-start(bf16[8,64,512]{2,1,0:T(8,128)(2,1)S(1)} %collective-permute-done.12.refs_2_.refs_11_), channel_id=1, source_target_pairs={{0,16},{8,120},{128,144},{136,248},{256,272},{264,376},{384,400},{... | collective-permute-start | bytes 1572872 | tf_op jit(solution)/shard_map/ppermute | solution.py:41
  110.8 12.3 %collective-permute-start.21 = (bf16[512,512]{1,0:T(8,128)(2,1)S(1)}, bf16[512,512]{1,0:T(8,128)(2,1)S(1)}, u32[]{:S(2)}, u32[]{:S(2)}) collective-permute-start(bf16[512,512]{1,0:T(8,128)(2,1)S(1)} %project.3.own), channel_id=1, source_target_pairs={{0,8},{8,16},{16,24},{24,32},{32,40},{40,48},{48,56},{56,64},{64,7... | collective-permute-start | bytes 1572872 | tf_op jit(solution)/shard_map/ppermute | solution.py:47
  115.1 22.8 %collective-permute-start.20 = (bf16[512,512]{1,0:T(8,128)(2,1)S(1)}, bf16[512,512]{1,0:T(8,128)(2,1)S(1)}, u32[]{:S(2)}, u32[]{:S(2)}) collective-permute-start(bf16[512,512]{1,0:T(8,128)(2,1)S(1)} %project.3.own), channel_id=1, source_target_pairs={{0,16},{8,24},{16,32},{24,40},{32,48},{40,56},{48,64},{56,72},{64,... | collective-permute-start | bytes 1572872 | tf_op jit(solution)/shard_map/ppermute | solution.py:47
  141.2 9.1 %collective-permute-start.22 = (bf16[512,256]{1,0:T(8,128)(2,1)S(1)}, bf16[512,256]{1,0:T(8,128)(2,1)S(1)}, u32[]{:S(2)}, u32[]{:S(2)}) collective-permute-start(bf16[512,256]{1,0:T(8,128)(2,1)S(1)} %get-tuple-element.14), channel_id=1, source_target_pairs={{16,0},{24,8},{32,16},{40,24},{48,32},{56,40},{64,48},{72,56},{80,... | collective-permute-start | bytes 786440 | tf_op jit(solution)/shard_map/ppermute | solution.py:47
  143.1 8.8 %collective-permute-start.23 = (bf16[512,256]{1,0:T(8,128)(2,1)S(1)}, bf16[512,256]{1,0:T(8,128)(2,1)S(1)}, u32[]{:S(2)}, u32[]{:S(2)}) collective-permute-start(bf16[512,256]{1,0:T(8,128)(2,1)S(1)} %get-tuple-element.15), channel_id=1, source_target_pairs={{8,0},{16,8},{24,16},{32,24},{40,32},{48,40},{56,48},{64,56},{72,6... | collective-permute-start | bytes 786440 | tf_op jit(solution)/shard_map/ppermute | solution.py:47
  (3 other events, 71.9 us)
where the time goes:
time: 154 us; the launch traced here: 153 us
  starting transfers between devices  76 us (49%)
  waiting for transfers between devices  57.4 us (37%)
  Pallas kernels  12.2 us (8%)
  blocking collectives  3.65 us (2%)
  other arithmetic  1.72 us (1%)
    ppermute x20, starting transfers between devices, hop(): return lax.ppermute(block, BOTH, route)  66 us
    ppermute x20, waiting for transfers between devices, hop(): return lax.ppermute(block, BOTH, route)  36 us
    ppermute x4, waiting for transfers between devices, along_ctx(): return lax.ppermute(block, 'ctx', route)  21.4 us
    ppermute x4, starting transfers between devices, along_ctx(): return lax.ppermute(block, 'ctx', route)  10 us
    pallas_call x2, Pallas kernels, project(): pl.pallas_call(lambda *refs: project_body(*refs, scale=scale), out_shape=...  4.81 us
    all_gather x1, blocking collectives, gather_zcore(): lax.all_gather(line, 'ctx', axis=0, tiled=False, axis_index_groups=chips)  3.65 us
    pallas_call x1, Pallas kernels, attend(): pl.pallas_call(far_body, out_shape=(shape((4, REACH, TILE), BF), shape((r...  3.23 us
  transfers between devices with their start and end apart: 24, of which 15 were waited for; matrix products, arithmetic and copies ran while one was open for 0% of the time, Pallas kernels for 6%

commit v1 on v0

--- a/solution.py
+++ b/solution.py
@@ -47,50 +47,54 @@
     return lax.ppermute(block, "ctx", route)
 
 
-def project_body(t0, t1, t2, t3, p0, p1, p2, p3, own_ref, r1, r2, r3, r4, swapped, o_ref, *, scale):
+def project_body(*refs, slots, scale):
+    count = len(slots)
+    near, far = refs[:count], refs[count : 2 * count]
+    own_ref, r1, r2, r3, r4, swapped = refs[2 * count : 2 * count + 6]
+    *sums, o_ref = refs[2 * count + 6 :]
     ctx = lax.axis_index("ctx").astype(jnp.int32)
     head = lax.axis_index("head").astype(jnp.int32)
     y = lax.rem(lax.div(ctx, 2), NY)
-    own_z = lax.div(ctx, 2 * NY)
     sign = 1 - 2 * lax.rem(ctx, 2)
     x, zh = lax.div(head, NZH), lax.rem(head, NZH)
-    total = jnp.zeros(o_ref.shape, F32)
-
-    for slot, (near, far) in enumerate(((t0, p0), (t1, p1), (t2, p2), (t3, p3))):
+    total = sums[0][...] if sums else jnp.zeros(o_ref.shape, F32)
+
+    for slot, near_ref, far_ref in zip(slots, near, far):
         z = lax.rem(x - sign * slot + NX, NX)
 
         def columns(distance):
             chip = lax.rem(y + sign * distance + NY, NY)
             at = pl.multiple_of(lax.rem(chip, 4) * PAIR, PAIR)
-            return jnp.where(lax.div(chip, 4) == zh, near[:, pl.ds(at, PAIR)], far[:, pl.ds(at, PAIR)])
+            mine = near_ref[:, pl.ds(at, PAIR)]
+            return jnp.where(lax.div(chip, 4) == zh, mine, far_ref[:, pl.ds(at, PAIR)])
 
         left = [columns(d) for d in (0, 4, -1, 1, -2, 2, -3, 3)]
-        j = lax.bitwise_xor(z, own_z)
-        right = [own_ref[j], own_ref[NZL + j], r4[j], r4[NZL + j]]
+        right = [own_ref[z], own_ref[NZL + z], r4[z], r4[NZL + z]]
         for step, ref in enumerate((r1, r2, r3)):
-            at = 2 * NZL * step + j
-            right += [ref[j], ref[NZL + j], swapped[at], swapped[at + NZL]]
+            at = 2 * NZL * step + z
+            right += [ref[z], ref[NZL + z], swapped[at], swapped[at + NZL]]
         total += jnp.dot(
             jnp.concatenate(left, axis=1),
             jnp.concatenate(right, axis=0),
             preferred_element_type=F32,
         )
-    o_ref[...] = (total * scale).astype(BF)
-
-
-def project(near, far, ring, swapped, scale):
+    o_ref[...] = (total * scale).astype(o_ref.dtype)
+
+
+def project(near, far, ring, swapped, scale, slots=(0, 1, 2, 3), sums=(), dtype=BF):
     rows = near[0].shape[0]
     cols = ring[0].shape[-1]
     full = pl.BlockSpec(memory_space=pltpu.VMEM)
-    operands = [*near, *far, *ring, swapped]
+    operands = [near[i] for i in slots] + [far[i] for i in slots] + [*ring, swapped, *sums]
+    depth = 1024 * len(slots)
     return pl.pallas_call(
-        lambda *refs: project_body(*refs, scale=scale),
-        out_shape=jax.ShapeDtypeStruct((rows, cols), BF),
+        lambda *refs: project_body(*refs, slots=slots, scale=scale),
+        out_shape=jax.ShapeDtypeStruct((rows, cols), dtype),
         in_specs=[full] * len(operands),
         out_specs=full,
         cost_estimate=pl.CostEstimate(
-            flops=2 * rows * 4096 * cols,
-            bytes_accessed=2 * (rows * 4096 + cols * 4096 + rows * cols),
+            flops=2 * rows * depth * cols,
+            bytes_accessed=2 * (rows * depth + cols * depth + rows * cols),
             transcendentals=0,
         ),
         compiler_params=pltpu.CompilerParams(vmem_limit_bytes=20 * MIB),
@@ -134,12 +138,13 @@
 
 
 def gather_zcore(w):
-    w = w[None]
-    line = joined_blocks([w] + [hop(w, flip=j) for j in (1, 2, 3)])
-    chips = [
-        [z * 2 * NY + 2 * y + core for core in range(2)] for z in range(NZL) for y in range(NY)
-    ]
-    w = lax.all_gather(line, "ctx", axis=0, tiled=False, axis_index_groups=chips)
+    def index(z, y, core):
+        return z * 2 * NY + 2 * y + core
+
+    lines = [[index(z, y, core) for z in range(NZL)] for y in range(NY) for core in range(2)]
+    chips = [[index(z, y, core) for core in range(2)] for z in range(NZL) for y in range(NY)]
+    w = lax.all_gather(w, "ctx", axis=0, tiled=False, axis_index_groups=lines)
+    w = lax.all_gather(w, "ctx", axis=0, tiled=False, axis_index_groups=chips)
     return w.reshape((2 * NZL,) + w.shape[2:])
 
 
@@ -335,7 +340,8 @@
     qs = ring_y(w[..., kv_cols:])
     q_a = hop(joined_blocks(qs[1:4]), swap=1)
 
-    joined = project(near, far, kv, kv_a, 1.0)
+    sums = project(near, far, kv, kv_a, 1.0, slots=(0, 1, 3), dtype=F32)
+    joined = project(near, far, kv, kv_a, 1.0, slots=(2,), sums=(sums,))
     query = project(near, far, qs, q_a, 0.0625)
 
     e2 = along_ctx(joined, 2)

time: 154 us -> 169 us (1.097)
  the two profiles are of different devices: /device:TPU:199 before, /device:TPU:65 now
where the time goes in v1:
time: 169 us; the launch traced here: 168 us
  starting transfers between devices  84.7 us (50%)
  waiting for transfers between devices  47 us (28%)
  blocking collectives  20.9 us (12%)
  Pallas kernels  12.4 us (7%)
  other arithmetic  1.7 us (1%)
    ppermute x17, starting transfers between devices, hop(): return lax.ppermute(block, BOTH, route)  71.1 us
    ppermute x17, waiting for transfers between devices, hop(): return lax.ppermute(block, BOTH, route)  26.4 us
    ppermute x4, waiting for transfers between devices, along_ctx(): return lax.ppermute(block, 'ctx', route)  20.6 us
    all_gather x1, blocking collectives, gather_zcore(): w = lax.all_gather(w, 'ctx', axis=0, tiled=False, axis_index_groups=lines)  15.6 us
    ppermute x4, starting transfers between devices, along_ctx(): return lax.ppermute(block, 'ctx', route)  13.6 us
    all_gather x1, blocking collectives, gather_zcore(): w = lax.all_gather(w, 'ctx', axis=0, tiled=False, axis_index_groups=chips)  5.25 us
    pallas_call x3, Pallas kernels, project(): pl.pallas_call(lambda *refs: project_body(*refs, slots=slots, scale=scale...  5.03 us
  transfers between devices with their start and end apart: 21, of which 13 were waited for; matrix products, arithmetic and copies ran while one was open for 0% of the time, Pallas kernels for 5%

profile of v1, /device:TPU:65, one launch (start us, length us, event | category | flops | bytes accessed | tf_op | source)
XLA Modules:
  0.0 168.4 jit_solution(7360156237202488430)
XLA Ops:
  1.6 15.6 %all-gather.2 = bf16[4,60,1024]{2,1,0:T(8,128)(2,1)S(1)} all-gather(bf16[1,60,1024]{2,1,0:T(8,128)(2,1)S(1)} %maximum_bitcast_fusion), channel_id=2, replica_groups={{0,128,256,384},{8,136,264,392},{16,144,272,400},{24,152,280,408},{32,1..., dimensions={0}, use_global_device_ids=true | all-gather | bytes 614400 | tf_op jit(solution)/shard_map/all_gather | solution.py:146
  17.2 5.3 %all-gather.1 = bf16[8,60,1024]{2,1,0:T(8,128)(2,1)S(1)} all-gather(bf16[4,60,1024]{2,1,0:T(8,128)(2,1)S(1)} %all-gather.2), channel_id=3, replica_groups={{0,8},{16,24},{32,40},{48,56},{64,72},{80,88},{96,104},{112,120},{128,1..., dimensions={0}, use_global_device_ids=true | all-gather | bytes 1474560 | tf_op jit(solution)/shard_map/all_gather | solution.py:147
  22.6 5.1 %collective-permute-start.12 = (bf16[8,64,512]{2,1,0:T(8,128)(2,1)S(1)}, bf16[8,64,512]{2,1,0:T(8,128)(2,1)S(1)}, u32[]{:S(2)}, u32[]{:S(2)}) collective-permute-start(bf16[8,64,512]{2,1,0:T(8,128)(2,1)S(1)} %get-tuple-element.16.refs_6_.refs_2_), channel_id=1, source_target_pairs={{0,16},{8,120},{128,144},{136,248},{256,272},{264,376},{384,400},{... | collective-permute-start | bytes 1572872 | tf_op jit(solution)/shard_map/ppermute | solution.py:41
  27.7 3.0 %collective-permute-start.7 = (bf16[8,64,512]{2,1,0:T(8,128)(2,1)S(1)}, bf16[8,64,512]{2,1,0:T(8,128)(2,1)S(1)}, u32[]{:S(2)}, u32[]{:S(2)}) collective-permute-start(bf16[8,64,512]{2,1,0:T(8,128)(2,1)S(1)} %get-tuple-element.17.refs_8_), channel_id=1, source_target_pairs={{0,16},{8,120},{128,144},{136,248},{256,272},{264,376},{384,400},{... | collective-permute-start | bytes 1572872 | tf_op jit(solution)/shard_map/ppermute | solution.py:41
  30.7 3.1 %collective-permute-done.12.refs_0_.refs_7_.refs_3_ = bf16[8,64,512]{2,1,0:T(8,128)(2,1)S(1)} collective-permute-done((bf16[8,64,512]{2,1,0:T(8,128)(2,1)S(1)}, bf16[8,64,512]{2,1,0:T(8,128)(2,1)S(1)}, u32[]{:S(2)}, u32[]{:S(2)}) %collective-permute-start.12) | collective-permute-done | bytes 524320 | tf_op jit(solution)/shard_map/ppermute | solution.py:41
  33.8 5.0 %collective-permute-start.13 = (bf16[8,64,512]{2,1,0:T(8,128)(2,1)S(1)}, bf16[8,64,512]{2,1,0:T(8,128)(2,1)S(1)}, u32[]{:S(2)}, u32[]{:S(2)}) collective-permute-start(bf16[8,64,512]{2,1,0:T(8,128)(2,1)S(1)} %collective-permute-done.12.refs_0_.refs_7_.refs_3_), channel_id=1, source_target_pairs={{0,16},{8,120},{128,144},{136,248},{256,272},{264,376},{384,400},{... | collective-permute-start | bytes 1572872 | tf_op jit(solution)/shard_map/ppermute | solution.py:41
  39.4 5.0 %collective-permute-start.8 = (bf16[8,64,512]{2,1,0:T(8,128)(2,1)S(1)}, bf16[8,64,512]{2,1,0:T(8,128)(2,1)S(1)}, u32[]{:S(2)}, u32[]{:S(2)}) collective-permute-start(bf16[8,64,512]{2,1,0:T(8,128)(2,1)S(1)} %collective-permute-done.7.refs_0_.refs_9_), channel_id=1, source_target_pairs={{0,16},{8,120},{128,144},{136,248},{256,272},{264,376},{384,400},{... | collective-permute-start | bytes 1572872 | tf_op jit(solution)/shard_map/ppermute | solution.py:41
  45.0 5.0 %collective-permute-start.14 = (bf16[8,64,512]{2,1,0:T(8,128)(2,1)S(1)}, bf16[8,64,512]{2,1,0:T(8,128)(2,1)S(1)}, u32[]{:S(2)}, u32[]{:S(2)}) collective-permute-start(bf16[8,64,512]{2,1,0:T(8,128)(2,1)S(1)} %collective-permute-done.13.refs_1_.refs_8_.refs_4_), channel_id=1, source_target_pairs={{0,16},{8,120},{128,144},{136,248},{256,272},{264,376},{384,400},{... | collective-permute-start | bytes 1572872 | tf_op jit(solution)/shard_map/ppermute | solution.py:41
  50.6 5.0 %collective-permute-start.9 = (bf16[8,64,512]{2,1,0:T(8,128)(2,1)S(1)}, bf16[8,64,512]{2,1,0:T(8,128)(2,1)S(1)}, u32[]{:S(2)}, u32[]{:S(2)}) collective-permute-start(bf16[8,64,512]{2,1,0:T(8,128)(2,1)S(1)} %collective-permute-done.8.refs_1_.refs_10_), channel_id=1, source_target_pairs={{0,16},{8,120},{128,144},{136,248},{256,272},{264,376},{384,400},{... | collective-permute-start | bytes 1572872 | tf_op jit(solution)/shard_map/ppermute | solution.py:41
  56.4 5.7 %collective-permute-start.16 = (bf16[24,64,512]{2,1,0:T(8,128)(2,1)S(1)}, bf16[24,64,512]{2,1,0:T(8,128)(2,1)S(1)}, u32[]{:S(2)}, u32[]{:S(2)}) collective-permute-start(bf16[24,64,512]{2,1,0:T(8,128)(2,1)S(1)} %join.3), channel_id=1, source_target_pairs={{0,8},{8,0},{128,136},{136,128},{256,264},{264,256},{384,392},{392... | collective-permute-start | bytes 4718600 | tf_op jit(solution)/shard_map/ppermute | solution.py:41
  62.6 7.9 %collective-permute-start.3 = (bf16[512,512]{1,0:T(8,128)(2,1)S(1)}, bf16[512,512]{1,0:T(8,128)(2,1)S(1)}, u32[]{:S(2)}, u32[]{:S(2)}) collective-permute-start(bf16[512,512]{1,0:T(8,128)(2,1)S(1)} %fusion.refs_0_), channel_id=1, source_target_pairs={{0,1},{8,9},{128,129},{136,137},{256,257},{264,265},{384,385},{392... | collective-permute-start | bytes 1572872 | tf_op jit(solution)/shard_map/ppermute | solution.py:41
  70.6 3.1 %collective-permute-start.2 = (bf16[512,512]{1,0:T(8,128)(2,1)S(1)}, bf16[512,512]{1,0:T(8,128)(2,1)S(1)}, u32[]{:S(2)}, u32[]{:S(2)}) collective-permute-start(bf16[512,512]{1,0:T(8,128)(2,1)S(1)} %fusion.refs_0_), channel_id=1, source_target_pairs={{0,6},{8,10},{128,134},{136,138},{256,262},{264,266},{384,390},{39... | collective-permute-start | bytes 1572872 | tf_op jit(solution)/shard_map/ppermute | solution.py:41
  73.7 3.4 %collective-permute-start = (bf16[512,512]{1,0:T(8,128)(2,1)S(1)}, bf16[512,512]{1,0:T(8,128)(2,1)S(1)}, u32[]{:S(2)}, u32[]{:S(2)}) collective-permute-start(bf16[512,512]{1,0:T(8,128)(2,1)S(1)} %fusion.refs_0_), channel_id=1, source_target_pairs={{0,2},{8,14},{128,130},{136,142},{256,258},{264,270},{384,386},{39... | collective-permute-start | bytes 1572872 | tf_op jit(solution)/shard_map/ppermute | solution.py:41
  79.5 14.6 %collective-permute-done.3.refs_4_.refs_3_ = bf16[512,512]{1,0:T(8,128)(2,1)S(1)} collective-permute-done((bf16[512,512]{1,0:T(8,128)(2,1)S(1)}, bf16[512,512]{1,0:T(8,128)(2,1)S(1)}, u32[]{:S(2)}, u32[]{:S(2)}) %collective-permute-start.3) | collective-permute-done | bytes 524320 | tf_op jit(solution)/shard_map/ppermute | solution.py:41
  94.1 3.1 %collective-permute-start.6 = (bf16[512,512]{1,0:T(8,128)(2,1)S(1)}, bf16[512,512]{1,0:T(8,128)(2,1)S(1)}, u32[]{:S(2)}, u32[]{:S(2)}) collective-permute-start(bf16[512,512]{1,0:T(8,128)(2,1)S(1)} %collective-permute-done.3.refs_4_.refs_3_), channel_id=1, source_target_pairs={{0,6},{8,10},{128,134},{136,138},{256,262},{264,266},{384,390},{39... | collective-permute-start | bytes 1572872 | tf_op jit(solution)/shard_map/ppermute | solution.py:41
  97.3 3.3 %collective-permute-start.4 = (bf16[512,512]{1,0:T(8,128)(2,1)S(1)}, bf16[512,512]{1,0:T(8,128)(2,1)S(1)}, u32[]{:S(2)}, u32[]{:S(2)}) collective-permute-start(bf16[512,512]{1,0:T(8,128)(2,1)S(1)} %collective-permute-done.3.refs_4_.refs_3_), channel_id=1, source_target_pairs={{0,2},{8,14},{128,130},{136,142},{256,258},{264,270},{384,386},{39... | collective-permute-start | bytes 1572872 | tf_op jit(solution)/shard_map/ppermute | solution.py:41
  105.3 5.0 %collective-permute-start.1 = (bf16[512,512]{1,0:T(8,128)(2,1)S(1)}, bf16[512,512]{1,0:T(8,128)(2,1)S(1)}, u32[]{:S(2)}, u32[]{:S(2)}) collective-permute-start(bf16[512,512]{1,0:T(8,128)(2,1)S(1)} %collective-permute-done.refs_1_), channel_id=1, source_target_pairs={{0,2},{8,14},{128,130},{136,142},{256,258},{264,270},{384,386},{39... | collective-permute-start | bytes 1572872 | tf_op jit(solution)/shard_map/ppermute | solution.py:41
  111.6 5.3 %collective-permute-start.5 = (bf16[512,512]{1,0:T(8,128)(2,1)S(1)}, bf16[512,512]{1,0:T(8,128)(2,1)S(1)}, u32[]{:S(2)}, u32[]{:S(2)}) collective-permute-start(bf16[512,512]{1,0:T(8,128)(2,1)S(1)} %collective-permute-done.4.refs_5_.refs_4_), channel_id=1, source_target_pairs={{0,2},{8,14},{128,130},{136,142},{256,258},{264,270},{384,386},{39... | collective-permute-start | bytes 1572872 | tf_op jit(solution)/shard_map/ppermute | solution.py:41
  123.8 7.0 %collective-permute-start.18 = (bf16[512,512]{1,0:T(8,128)(2,1)S(1)}, bf16[512,512]{1,0:T(8,128)(2,1)S(1)}, u32[]{:S(2)}, u32[]{:S(2)}) collective-permute-start(bf16[512,512]{1,0:T(8,128)(2,1)S(1)} %project.5.own), channel_id=1, source_target_pairs={{0,8},{8,16},{16,24},{24,32},{32,40},{40,48},{48,56},{56,64},{64,7... | collective-permute-start | bytes 1572872 | tf_op jit(solution)/shard_map/ppermute | solution.py:47
  130.8 2.7 %collective-permute-start.17 = (bf16[512,512]{1,0:T(8,128)(2,1)S(1)}, bf16[512,512]{1,0:T(8,128)(2,1)S(1)}, u32[]{:S(2)}, u32[]{:S(2)}) collective-permute-start(bf16[512,512]{1,0:T(8,128)(2,1)S(1)} %project.5.own), channel_id=1, source_target_pairs={{0,16},{8,24},{16,32},{24,40},{32,48},{40,56},{48,64},{56,72},{64,... | collective-permute-start | bytes 1572872 | tf_op jit(solution)/shard_map/ppermute | solution.py:47
  136.0 2.8 %collective-permute-done.18.e1 = bf16[512,512]{1,0:T(8,128)(2,1)S(1)} collective-permute-done((bf16[512,512]{1,0:T(8,128)(2,1)S(1)}, bf16[512,512]{1,0:T(8,128)(2,1)S(1)}, u32[]{:S(2)}, u32[]{:S(2)}) %collective-permute-start.18) | collective-permute-done | bytes 524320 | tf_op jit(solution)/shard_map/ppermute | solution.py:47
  141.0 12.6 %collective-permute-done.17.e2 = bf16[512,512]{1,0:T(8,128)(2,1)S(1)} collective-permute-done((bf16[512,512]{1,0:T(8,128)(2,1)S(1)}, bf16[512,512]{1,0:T(8,128)(2,1)S(1)}, u32[]{:S(2)}, u32[]{:S(2)}) %collective-permute-start.17) | collective-permute-done | bytes 524320 | tf_op jit(solution)/shard_map/ppermute | solution.py:47
  153.6 3.2 %far_scores.1 = (bf16[4,1280,256]{2,1,0:T(8,128)(2,1)S(1)}, f32[512,256]{1,0:T(8,128)S(1)}, bf16[512,256]{1,0:T(8,128)(2,1)S(1)}, bf16[512,256]{1,0:T(8,128)(2,1)S(1)}) custom-call(s32[1,32]{1,0:T(1,128)S(1)} %bitcast.7, bf16[512,512]{1,0:T(8,128)(2,1)S(1)} %project.3.q_ref, bf16[512,512]{1,0:T(8,128)(2,1)S(1)} %collective-permute-done.17.e2, ...), custom_call_target="tpu_custom_call" | custom-call | flops 1006632960 | bytes 15728640 | tf_op jit(solution)/shard_map/far_scores/pallas_call | solution.py:290
  162.4 3.5 %collective-permute-done.19 = bf16[512,256]{1,0:T(8,128)(2,1)S(1)} collective-permute-done((bf16[512,256]{1,0:T(8,128)(2,1)S(1)}, bf16[512,256]{1,0:T(8,128)(2,1)S(1)}, u32[]{:S(2)}, u32[]{:S(2)}) %collective-permute-start.19) | collective-permute-done | bytes 262176 | tf_op jit(solution)/shard_map/ppermute | solution.py:47
  (39 shorter events, 32.0 us)
Async XLA Ops:
  0.6 61.4 %copy-start = (bf16[512,480]{0,1:T(8,128)(2,1)S(1)}, bf16[512,480]{0,1:T(8,128)(2,1)}, u32[]{:S(2)}) copy-start(bf16[512,480]{0,1:T(8,128)(2,1)} %param.6) | copy-start | bytes 1474564
  22.6 11.2 %collective-permute-start.12 = (bf16[8,64,512]{2,1,0:T(8,128)(2,1)S(1)}, bf16[8,64,512]{2,1,0:T(8,128)(2,1)S(1)}, u32[]{:S(2)}, u32[]{:S(2)}) collective-permute-start(bf16[8,64,512]{2,1,0:T(8,128)(2,1)S(1)} %get-tuple-element.16.refs_6_.refs_2_), channel_id=1, source_target_pairs={{0,16},{8,120},{128,144},{136,248},{256,272},{264,376},{384,400},{... | collective-permute-start | bytes 1572872 | tf_op jit(solution)/shard_map/ppermute | solution.py:41
  27.7 11.7 %collective-permute-start.7 = (bf16[8,64,512]{2,1,0:T(8,128)(2,1)S(1)}, bf16[8,64,512]{2,1,0:T(8,128)(2,1)S(1)}, u32[]{:S(2)}, u32[]{:S(2)}) collective-permute-start(bf16[8,64,512]{2,1,0:T(8,128)(2,1)S(1)} %get-tuple-element.17.refs_8_), channel_id=1, source_target_pairs={{0,16},{8,120},{128,144},{136,248},{256,272},{264,376},{384,400},{... | collective-permute-start | bytes 1572872 | tf_op jit(solution)/shard_map/ppermute | solution.py:41
  33.8 11.2 %collective-permute-start.13 = (bf16[8,64,512]{2,1,0:T(8,128)(2,1)S(1)}, bf16[8,64,512]{2,1,0:T(8,128)(2,1)S(1)}, u32[]{:S(2)}, u32[]{:S(2)}) collective-permute-start(bf16[8,64,512]{2,1,0:T(8,128)(2,1)S(1)} %collective-permute-done.12.refs_0_.refs_7_.refs_3_), channel_id=1, source_target_pairs={{0,16},{8,120},{128,144},{136,248},{256,272},{264,376},{384,400},{... | collective-permute-start | bytes 1572872 | tf_op jit(solution)/shard_map/ppermute | solution.py:41
  39.4 11.2 %collective-permute-start.8 = (bf16[8,64,512]{2,1,0:T(8,128)(2,1)S(1)}, bf16[8,64,512]{2,1,0:T(8,128)(2,1)S(1)}, u32[]{:S(2)}, u32[]{:S(2)}) collective-permute-start(bf16[8,64,512]{2,1,0:T(8,128)(2,1)S(1)} %collective-permute-done.7.refs_0_.refs_9_), channel_id=1, source_target_pairs={{0,16},{8,120},{128,144},{136,248},{256,272},{264,376},{384,400},{... | collective-permute-start | bytes 1572872 | tf_op jit(solution)/shard_map/ppermute | solution.py:41
  45.0 11.2 %collective-permute-start.14 = (bf16[8,64,512]{2,1,0:T(8,128)(2,1)S(1)}, bf16[8,64,512]{2,1,0:T(8,128)(2,1)S(1)}, u32[]{:S(2)}, u32[]{:S(2)}) collective-permute-start(bf16[8,64,512]{2,1,0:T(8,128)(2,1)S(1)} %collective-permute-done.13.refs_1_.refs_8_.refs_4_), channel_id=1, source_target_pairs={{0,16},{8,120},{128,144},{136,248},{256,272},{264,376},{384,400},{... | collective-permute-start | bytes 1572872 | tf_op jit(solution)/shard_map/ppermute | solution.py:41
  50.6 26.5 %collective-permute-start.9 = (bf16[8,64,512]{2,1,0:T(8,128)(2,1)S(1)}, bf16[8,64,512]{2,1,0:T(8,128)(2,1)S(1)}, u32[]{:S(2)}, u32[]{:S(2)}) collective-permute-start(bf16[8,64,512]{2,1,0:T(8,128)(2,1)S(1)} %collective-permute-done.8.refs_1_.refs_10_), channel_id=1, source_target_pairs={{0,16},{8,120},{128,144},{136,248},{256,272},{264,376},{384,400},{... | collective-permute-start | bytes 1572872 | tf_op jit(solution)/shard_map/ppermute | solution.py:41
  56.4 62.5 %collective-permute-start.16 = (bf16[24,64,512]{2,1,0:T(8,128)(2,1)S(1)}, bf16[24,64,512]{2,1,0:T(8,128)(2,1)S(1)}, u32[]{:S(2)}, u32[]{:S(2)}) collective-permute-start(bf16[24,64,512]{2,1,0:T(8,128)(2,1)S(1)} %join.3), channel_id=1, source_target_pairs={{0,8},{8,0},{128,136},{136,128},{256,264},{264,256},{384,392},{392... | collective-permute-start | bytes 4718600 | tf_op jit(solution)/shard_map/ppermute | solution.py:41
  62.6 31.5 %collective-permute-start.3 = (bf16[512,512]{1,0:T(8,128)(2,1)S(1)}, bf16[512,512]{1,0:T(8,128)(2,1)S(1)}, u32[]{:S(2)}, u32[]{:S(2)}) collective-permute-start(bf16[512,512]{1,0:T(8,128)(2,1)S(1)} %fusion.refs_0_), channel_id=1, source_target_pairs={{0,1},{8,9},{128,129},{136,137},{256,257},{264,265},{384,385},{392... | collective-permute-start | bytes 1572872 | tf_op jit(solution)/shard_map/ppermute | solution.py:41
  70.6 26.7 %collective-permute-start.2 = (bf16[512,512]{1,0:T(8,128)(2,1)S(1)}, bf16[512,512]{1,0:T(8,128)(2,1)S(1)}, u32[]{:S(2)}, u32[]{:S(2)}) collective-permute-start(bf16[512,512]{1,0:T(8,128)(2,1)S(1)} %fusion.refs_0_), channel_id=1, source_target_pairs={{0,6},{8,10},{128,134},{136,138},{256,262},{264,266},{384,390},{39... | collective-permute-start | bytes 1572872 | tf_op jit(solution)/shard_map/ppermute | solution.py:41
  73.7 26.9 %collective-permute-start = (bf16[512,512]{1,0:T(8,128)(2,1)S(1)}, bf16[512,512]{1,0:T(8,128)(2,1)S(1)}, u32[]{:S(2)}, u32[]{:S(2)}) collective-permute-start(bf16[512,512]{1,0:T(8,128)(2,1)S(1)} %fusion.refs_0_), channel_id=1, source_target_pairs={{0,2},{8,14},{128,130},{136,142},{256,258},{264,270},{384,386},{39... | collective-permute-start | bytes 1572872 | tf_op jit(solution)/shard_map/ppermute | solution.py:41
  77.2 56.3 %collective-permute-start.11 = (bf16[24,64,512]{2,1,0:T(8,128)(2,1)S(1)}, bf16[24,64,512]{2,1,0:T(8,128)(2,1)S(1)}, u32[]{:S(2)}, u32[]{:S(2)}) collective-permute-start(bf16[24,64,512]{2,1,0:T(8,128)(2,1)S(1)} %join.2), channel_id=1, source_target_pairs={{0,8},{8,0},{128,136},{136,128},{256,264},{264,256},{384,392},{392... | collective-permute-start | bytes 4718600 | tf_op jit(solution)/shard_map/ppermute | solution.py:41
  94.1 11.1 %collective-permute-start.6 = (bf16[512,512]{1,0:T(8,128)(2,1)S(1)}, bf16[512,512]{1,0:T(8,128)(2,1)S(1)}, u32[]{:S(2)}, u32[]{:S(2)}) collective-permute-start(bf16[512,512]{1,0:T(8,128)(2,1)S(1)} %collective-permute-done.3.refs_4_.refs_3_), channel_id=1, source_target_pairs={{0,6},{8,10},{128,134},{136,138},{256,262},{264,266},{384,390},{39... | collective-permute-start | bytes 1572872 | tf_op jit(solution)/shard_map/ppermute | solution.py:41
  97.3 14.3 %collective-permute-start.4 = (bf16[512,512]{1,0:T(8,128)(2,1)S(1)}, bf16[512,512]{1,0:T(8,128)(2,1)S(1)}, u32[]{:S(2)}, u32[]{:S(2)}) collective-permute-start(bf16[512,512]{1,0:T(8,128)(2,1)S(1)} %collective-permute-done.3.refs_4_.refs_3_), channel_id=1, source_target_pairs={{0,2},{8,14},{128,130},{136,142},{256,258},{264,270},{384,386},{39... | collective-permute-start | bytes 1572872 | tf_op jit(solution)/shard_map/ppermute | solution.py:41
  100.7 16.3 %collective-permute-start.15 = (bf16[8,64,512]{2,1,0:T(8,128)(2,1)S(1)}, bf16[8,64,512]{2,1,0:T(8,128)(2,1)S(1)}, u32[]{:S(2)}, u32[]{:S(2)}) collective-permute-start(bf16[8,64,512]{2,1,0:T(8,128)(2,1)S(1)} %collective-permute-done.14.refs_2_.refs_9_.refs_5_), channel_id=1, source_target_pairs={{0,16},{8,120},{128,144},{136,248},{256,272},{264,376},{384,400},{... | collective-permute-start | bytes 1572872 | tf_op jit(solution)/shard_map/ppermute | solution.py:41
  105.3 15.5 %collective-permute-start.1 = (bf16[512,512]{1,0:T(8,128)(2,1)S(1)}, bf16[512,512]{1,0:T(8,128)(2,1)S(1)}, u32[]{:S(2)}, u32[]{:S(2)}) collective-permute-start(bf16[512,512]{1,0:T(8,128)(2,1)S(1)} %collective-permute-done.refs_1_), channel_id=1, source_target_pairs={{0,2},{8,14},{128,130},{136,142},{256,258},{264,270},{384,386},{39... | collective-permute-start | bytes 1572872 | tf_op jit(solution)/shard_map/ppermute | solution.py:41
  111.6 11.4 %collective-permute-start.5 = (bf16[512,512]{1,0:T(8,128)(2,1)S(1)}, bf16[512,512]{1,0:T(8,128)(2,1)S(1)}, u32[]{:S(2)}, u32[]{:S(2)}) collective-permute-start(bf16[512,512]{1,0:T(8,128)(2,1)S(1)} %collective-permute-done.4.refs_5_.refs_4_), channel_id=1, source_target_pairs={{0,2},{8,14},{128,130},{136,142},{256,258},{264,270},{384,386},{39... | collective-permute-start | bytes 1572872 | tf_op jit(solution)/shard_map/ppermute | solution.py:41
  116.9 16.6 %collective-permute-start.10 = (bf16[8,64,512]{2,1,0:T(8,128)(2,1)S(1)}, bf16[8,64,512]{2,1,0:T(8,128)(2,1)S(1)}, u32[]{:S(2)}, u32[]{:S(2)}) collective-permute-start(bf16[8,64,512]{2,1,0:T(8,128)(2,1)S(1)} %collective-permute-done.9.refs_2_.refs_11_), channel_id=1, source_target_pairs={{0,16},{8,120},{128,144},{136,248},{256,272},{264,376},{384,400},{... | collective-permute-start | bytes 1572872 | tf_op jit(solution)/shard_map/ppermute | solution.py:41
  123.7 15.0 %copy-start.1 = (bf16[512,512]{1,0:T(8,128)(2,1)S(1)}, bf16[512,512]{1,0:T(8,128)(2,1)}, u32[]{:S(2)}) copy-start(bf16[512,512]{1,0:T(8,128)(2,1)} %g_ref.3) | copy-start | bytes 1572868
  123.7 15.0 %copy-start.2 = (s32[32]{0:T(128)S(1)}, s32[32]{0:T(128)}, u32[]{:S(2)}) copy-start(s32[32]{0:T(128)} %param.11) | copy-start | bytes 388
  123.8 15.0 %collective-permute-start.18 = (bf16[512,512]{1,0:T(8,128)(2,1)S(1)}, bf16[512,512]{1,0:T(8,128)(2,1)S(1)}, u32[]{:S(2)}, u32[]{:S(2)}) collective-permute-start(bf16[512,512]{1,0:T(8,128)(2,1)S(1)} %project.5.own), channel_id=1, source_target_pairs={{0,8},{8,16},{16,24},{24,32},{32,40},{40,48},{48,56},{56,64},{64,7... | collective-permute-start | bytes 1572872 | tf_op jit(solution)/shard_map/ppermute | solution.py:47
  130.8 22.8 %collective-permute-start.17 = (bf16[512,512]{1,0:T(8,128)(2,1)S(1)}, bf16[512,512]{1,0:T(8,128)(2,1)S(1)}, u32[]{:S(2)}, u32[]{:S(2)}) collective-permute-start(bf16[512,512]{1,0:T(8,128)(2,1)S(1)} %project.5.own), channel_id=1, source_target_pairs={{0,16},{8,24},{16,32},{24,40},{32,48},{40,56},{48,64},{56,72},{64,... | collective-permute-start | bytes 1572872 | tf_op jit(solution)/shard_map/ppermute | solution.py:47
  156.9 9.0 %collective-permute-start.19 = (bf16[512,256]{1,0:T(8,128)(2,1)S(1)}, bf16[512,256]{1,0:T(8,128)(2,1)S(1)}, u32[]{:S(2)}, u32[]{:S(2)}) collective-permute-start(bf16[512,256]{1,0:T(8,128)(2,1)S(1)} %get-tuple-element.14), channel_id=1, source_target_pairs={{16,0},{24,8},{32,16},{40,24},{48,32},{56,40},{64,48},{72,56},{80,... | collective-permute-start | bytes 786440 | tf_op jit(solution)/shard_map/ppermute | solution.py:47
  158.8 8.8 %collective-permute-start.20 = (bf16[512,256]{1,0:T(8,128)(2,1)S(1)}, bf16[512,256]{1,0:T(8,128)(2,1)S(1)}, u32[]{:S(2)}, u32[]{:S(2)}) collective-permute-start(bf16[512,256]{1,0:T(8,128)(2,1)S(1)} %get-tuple-element.15), channel_id=1, source_target_pairs={{8,0},{16,8},{24,16},{32,24},{40,32},{48,40},{56,48},{64,56},{72,6... | collective-permute-start | bytes 786440 | tf_op jit(solution)/shard_map/ppermute | solution.py:47

commit v2 on v1

--- a/solution.py
+++ b/solution.py
@@ -102,9 +102,29 @@
     )(*operands)
 
 
-def ring_y(block):
-    out = [block]
-    for _ in range(4):
+def split_body(w_ref, kv_ref, q_ref):
+    cols = kv_ref.shape[-1]
+    kv_ref[...] = w_ref[:, :, :cols]
+    q_ref[...] = w_ref[:, :, cols:]
+
+
+def split(w):
+    full = pl.BlockSpec(memory_space=pltpu.VMEM)
+    half = jax.ShapeDtypeStruct(w.shape[:2] + (2 * HEAD_SIZE,), BF)
+    return pl.pallas_call(
+        split_body,
+        out_shape=(half, half),
+        in_specs=[full],
+        out_specs=(full, full),
+        cost_estimate=pl.CostEstimate(flops=0, bytes_accessed=4 * 2**20, transcendentals=0),
+        compiler_params=pltpu.CompilerParams(vmem_limit_bytes=8 * MIB),
+        name="split",
+    )(w)
+
+
+def ring_y(block, first):
+    out = [block, first]
+    for _ in range(1, 4):
         out.append(hop(out[-1], dy=1, by_core=True))
     return out
 
@@ -334,10 +354,11 @@
 
     w = gather_zcore(jnp.concatenate([key_matrix, value_matrix, w_query], axis=1))
     w = jnp.pad(w, ((0, 0), (0, PAD - ROWS), (0, 0)))
-    kv_cols = 2 * HEAD_SIZE
-    kv = ring_y(w[..., :kv_cols])
+    kv_own, q_own = split(w)
+    kv_one, q_one = split(hop(w, dy=1, by_core=True))
+    kv = ring_y(kv_own, kv_one)
     kv_a = hop(joined_blocks(kv[1:4]), swap=1)
-    qs = ring_y(w[..., kv_cols:])
+    qs = ring_y(q_own, q_one)
     q_a = hop(joined_blocks(qs[1:4]), swap=1)
 
     sums = project(near, far, kv, kv_a, 1.0, slots=(0, 1, 3), dtype=F32)

time: 169 us -> 175 us (1.036)
  waiting for transfers between devices: 47 us -> 58.3 us
  starting transfers between devices: 84.7 us -> 78.7 us
    ppermute x17 -> x16, waiting for transfers between devices: 26.4 us -> 37.8 us  [hop(): return lax.ppermute(block, BOTH, route)]
    ppermute x17 -> x16, starting transfers between devices: 71.1 us -> 65.3 us  [hop(): return lax.ppermute(block, BOTH, route)]
  transfers between devices with their start and end apart: 21 -> 20, of which waited for: 13 -> 12; matrix products, arithmetic and copies ran while one was open for 0% -> 0% of each run, Pallas kernels for 5% -> 5%
where the time goes in v2:
time: 175 us; the launch traced here: 174 us
  starting transfers between devices  78.7 us (45%)
  waiting for transfers between devices  58.3 us (33%)
  blocking collectives  20.9 us (12%)
  Pallas kernels  12.6 us (7%)
    ppermute x16, starting transfers between devices, hop(): return lax.ppermute(block, BOTH, route)  65.3 us
    ppermute x16, waiting for transfers between devices, hop(): return lax.ppermute(block, BOTH, route)  37.8 us
    ppermute x4, waiting for transfers between devices, along_ctx(): return lax.ppermute(block, 'ctx', route)  20.6 us
    all_gather x1, blocking collectives, gather_zcore(): w = lax.all_gather(w, 'ctx', axis=0, tiled=False, axis_index_groups=lines)  15.6 us
    ppermute x4, starting transfers between devices, along_ctx(): return lax.ppermute(block, 'ctx', route)  13.4 us
    all_gather x1, blocking collectives, gather_zcore(): w = lax.all_gather(w, 'ctx', axis=0, tiled=False, axis_index_groups=chips)  5.25 us
    pallas_call x3, Pallas kernels, project(): pl.pallas_call(lambda *refs: project_body(*refs, slots=slots, scale=scale...  5.02 us
  transfers between devices with their start and end apart: 20, of which 12 were waited for; matrix products, arithmetic and copies ran while one was open for 0% of the time, Pallas kernels for 5%

profile of v2, /device:TPU:65, one launch (start us, length us, event | category | flops | bytes accessed | tf_op | source)
XLA Modules:
  0.0 173.9 jit_solution(15940521020194820682)
XLA Ops:
  1.6 15.6 %all-gather.2 = bf16[4,60,1024]{2,1,0:T(8,128)(2,1)S(1)} all-gather(bf16[1,60,1024]{2,1,0:T(8,128)(2,1)S(1)} %maximum_bitcast_fusion), channel_id=2, replica_groups={{0,128,256,384},{8,136,264,392},{16,144,272,400},{24,152,280,408},{32,1..., dimensions={0}, use_global_device_ids=true | all-gather | bytes 614400 | tf_op jit(solution)/shard_map/all_gather | solution.py:166
  17.2 5.3 %all-gather.1 = bf16[8,60,1024]{2,1,0:T(8,128)(2,1)S(1)} all-gather(bf16[4,60,1024]{2,1,0:T(8,128)(2,1)S(1)} %all-gather.2), channel_id=3, replica_groups={{0,8},{16,24},{32,40},{48,56},{64,72},{80,88},{96,104},{112,120},{128,1..., dimensions={0}, use_global_device_ids=true | all-gather | bytes 1474560 | tf_op jit(solution)/shard_map/all_gather | solution.py:167
  22.6 5.1 %collective-permute-start.7 = (bf16[8,64,1024]{2,1,0:T(8,128)(2,1)S(1)}, bf16[8,64,1024]{2,1,0:T(8,128)(2,1)S(1)}, u32[]{:S(2)}, u32[]{:S(2)}) collective-permute-start(bf16[8,64,1024]{2,1,0:T(8,128)(2,1)S(1)} %pad.4.w_ref), channel_id=1, source_target_pairs={{0,16},{8,120},{128,144},{136,248},{256,272},{264,376},{384,400},{... | collective-permute-start | bytes 3145736 | tf_op jit(solution)/shard_map/ppermute | solution.py:41
  27.7 11.7 %collective-permute-done.7.w_ref = bf16[8,64,1024]{2,1,0:T(8,128)(2,1)S(1)} collective-permute-done((bf16[8,64,1024]{2,1,0:T(8,128)(2,1)S(1)}, bf16[8,64,1024]{2,1,0:T(8,128)(2,1)S(1)}, u32[]{:S(2)}, u32[]{:S(2)}) %collective-permute-start.7) | collective-permute-done | bytes 1048608 | tf_op jit(solution)/shard_map/ppermute | solution.py:41
  39.5 5.0 %collective-permute-start.12 = (bf16[8,64,512]{2,1,0:T(8,128)(2,1)S(1)}, bf16[8,64,512]{2,1,0:T(8,128)(2,1)S(1)}, u32[]{:S(2)}, u32[]{:S(2)}) collective-permute-start(bf16[8,64,512]{2,1,0:T(8,128)(2,1)S(1)} %get-tuple-element.16.refs_0_.refs_7_.refs_3_), channel_id=1, source_target_pairs={{0,16},{8,120},{128,144},{136,248},{256,272},{264,376},{384,400},{... | collective-permute-start | bytes 1572872 | tf_op jit(solution)/shard_map/ppermute | solution.py:41
  46.6 4.0 %collective-permute-done.12.refs_1_.refs_8_.refs_4_ = bf16[8,64,512]{2,1,0:T(8,128)(2,1)S(1)} collective-permute-done((bf16[8,64,512]{2,1,0:T(8,128)(2,1)S(1)}, bf16[8,64,512]{2,1,0:T(8,128)(2,1)S(1)}, u32[]{:S(2)}, u32[]{:S(2)}) %collective-permute-start.12) | collective-permute-done | bytes 524320 | tf_op jit(solution)/shard_map/ppermute | solution.py:41
  50.6 5.0 %collective-permute-start.13 = (bf16[8,64,512]{2,1,0:T(8,128)(2,1)S(1)}, bf16[8,64,512]{2,1,0:T(8,128)(2,1)S(1)}, u32[]{:S(2)}, u32[]{:S(2)}) collective-permute-start(bf16[8,64,512]{2,1,0:T(8,128)(2,1)S(1)} %collective-permute-done.12.refs_1_.refs_8_.refs_4_), channel_id=1, source_target_pairs={{0,16},{8,120},{128,144},{136,248},{256,272},{264,376},{384,400},{... | collective-permute-start | bytes 1572872 | tf_op jit(solution)/shard_map/ppermute | solution.py:41
  56.2 5.0 %collective-permute-start.9 = (bf16[8,64,512]{2,1,0:T(8,128)(2,1)S(1)}, bf16[8,64,512]{2,1,0:T(8,128)(2,1)S(1)}, u32[]{:S(2)}, u32[]{:S(2)}) collective-permute-start(bf16[8,64,512]{2,1,0:T(8,128)(2,1)S(1)} %collective-permute-done.8.refs_1_.refs_10_), channel_id=1, source_target_pairs={{0,16},{8,120},{128,144},{136,248},{256,272},{264,376},{384,400},{... | collective-permute-start | bytes 1572872 | tf_op jit(solution)/shard_map/ppermute | solution.py:41
  62.0 5.8 %collective-permute-start.15 = (bf16[24,64,512]{2,1,0:T(8,128)(2,1)S(1)}, bf16[24,64,512]{2,1,0:T(8,128)(2,1)S(1)}, u32[]{:S(2)}, u32[]{:S(2)}) collective-permute-start(bf16[24,64,512]{2,1,0:T(8,128)(2,1)S(1)} %join.3), channel_id=1, source_target_pairs={{0,8},{8,0},{128,136},{136,128},{256,264},{264,256},{384,392},{392... | collective-permute-start | bytes 4718600 | tf_op jit(solution)/shard_map/ppermute | solution.py:41
  68.3 7.9 %collective-permute-start.3 = (bf16[512,512]{1,0:T(8,128)(2,1)S(1)}, bf16[512,512]{1,0:T(8,128)(2,1)S(1)}, u32[]{:S(2)}, u32[]{:S(2)}) collective-permute-start(bf16[512,512]{1,0:T(8,128)(2,1)S(1)} %fusion.refs_0_), channel_id=1, source_target_pairs={{0,1},{8,9},{128,129},{136,137},{256,257},{264,265},{384,385},{392... | collective-permute-start | bytes 1572872 | tf_op jit(solution)/shard_map/ppermute | solution.py:41
  76.3 3.1 %collective-permute-start.2 = (bf16[512,512]{1,0:T(8,128)(2,1)S(1)}, bf16[512,512]{1,0:T(8,128)(2,1)S(1)}, u32[]{:S(2)}, u32[]{:S(2)}) collective-permute-start(bf16[512,512]{1,0:T(8,128)(2,1)S(1)} %fusion.refs_0_), channel_id=1, source_target_pairs={{0,6},{8,10},{128,134},{136,138},{256,262},{264,266},{384,390},{39... | collective-permute-start | bytes 1572872 | tf_op jit(solution)/shard_map/ppermute | solution.py:41
  79.4 3.4 %collective-permute-start = (bf16[512,512]{1,0:T(8,128)(2,1)S(1)}, bf16[512,512]{1,0:T(8,128)(2,1)S(1)}, u32[]{:S(2)}, u32[]{:S(2)}) collective-permute-start(bf16[512,512]{1,0:T(8,128)(2,1)S(1)} %fusion.refs_0_), channel_id=1, source_target_pairs={{0,2},{8,14},{128,130},{136,142},{256,258},{264,270},{384,386},{39... | collective-permute-start | bytes 1572872 | tf_op jit(solution)/shard_map/ppermute | solution.py:41
  85.2 14.6 %collective-permute-done.3.refs_4_.refs_3_ = bf16[512,512]{1,0:T(8,128)(2,1)S(1)} collective-permute-done((bf16[512,512]{1,0:T(8,128)(2,1)S(1)}, bf16[512,512]{1,0:T(8,128)(2,1)S(1)}, u32[]{:S(2)}, u32[]{:S(2)}) %collective-permute-start.3) | collective-permute-done | bytes 524320 | tf_op jit(solution)/shard_map/ppermute | solution.py:41
  99.8 3.1 %collective-permute-start.6 = (bf16[512,512]{1,0:T(8,128)(2,1)S(1)}, bf16[512,512]{1,0:T(8,128)(2,1)S(1)}, u32[]{:S(2)}, u32[]{:S(2)}) collective-permute-start(bf16[512,512]{1,0:T(8,128)(2,1)S(1)} %collective-permute-done.3.refs_4_.refs_3_), channel_id=1, source_target_pairs={{0,6},{8,10},{128,134},{136,138},{256,262},{264,266},{384,390},{39... | collective-permute-start | bytes 1572872 | tf_op jit(solution)/shard_map/ppermute | solution.py:41
  103.0 3.4 %collective-permute-start.4 = (bf16[512,512]{1,0:T(8,128)(2,1)S(1)}, bf16[512,512]{1,0:T(8,128)(2,1)S(1)}, u32[]{:S(2)}, u32[]{:S(2)}) collective-permute-start(bf16[512,512]{1,0:T(8,128)(2,1)S(1)} %collective-permute-done.3.refs_4_.refs_3_), channel_id=1, source_target_pairs={{0,2},{8,14},{128,130},{136,142},{256,258},{264,270},{384,386},{39... | collective-permute-start | bytes 1572872 | tf_op jit(solution)/shard_map/ppermute | solution.py:41
  108.3 2.7 %collective-permute-done.6.refs_7_.refs_5_ = bf16[512,512]{1,0:T(8,128)(2,1)S(1)} collective-permute-done((bf16[512,512]{1,0:T(8,128)(2,1)S(1)}, bf16[512,512]{1,0:T(8,128)(2,1)S(1)}, u32[]{:S(2)}, u32[]{:S(2)}) %collective-permute-start.6) | collective-permute-done | bytes 524320 | tf_op jit(solution)/shard_map/ppermute | solution.py:41
  111.0 5.0 %collective-permute-start.1 = (bf16[512,512]{1,0:T(8,128)(2,1)S(1)}, bf16[512,512]{1,0:T(8,128)(2,1)S(1)}, u32[]{:S(2)}, u32[]{:S(2)}) collective-permute-start(bf16[512,512]{1,0:T(8,128)(2,1)S(1)} %collective-permute-done.refs_1_), channel_id=1, source_target_pairs={{0,2},{8,14},{128,130},{136,142},{256,258},{264,270},{384,386},{39... | collective-permute-start | bytes 1572872 | tf_op jit(solution)/shard_map/ppermute | solution.py:41
  117.3 5.3 %collective-permute-start.5 = (bf16[512,512]{1,0:T(8,128)(2,1)S(1)}, bf16[512,512]{1,0:T(8,128)(2,1)S(1)}, u32[]{:S(2)}, u32[]{:S(2)}) collective-permute-start(bf16[512,512]{1,0:T(8,128)(2,1)S(1)} %collective-permute-done.4.refs_5_.refs_4_), channel_id=1, source_target_pairs={{0,2},{8,14},{128,130},{136,142},{256,258},{264,270},{384,386},{39... | collective-permute-start | bytes 1572872 | tf_op jit(solution)/shard_map/ppermute | solution.py:41
  129.4 6.9 %collective-permute-start.17 = (bf16[512,512]{1,0:T(8,128)(2,1)S(1)}, bf16[512,512]{1,0:T(8,128)(2,1)S(1)}, u32[]{:S(2)}, u32[]{:S(2)}) collective-permute-start(bf16[512,512]{1,0:T(8,128)(2,1)S(1)} %project.5.own), channel_id=1, source_target_pairs={{0,8},{8,16},{16,24},{24,32},{32,40},{40,48},{48,56},{56,64},{64,7... | collective-permute-start | bytes 1572872 | tf_op jit(solution)/shard_map/ppermute | solution.py:47
  136.3 2.7 %collective-permute-start.16 = (bf16[512,512]{1,0:T(8,128)(2,1)S(1)}, bf16[512,512]{1,0:T(8,128)(2,1)S(1)}, u32[]{:S(2)}, u32[]{:S(2)}) collective-permute-start(bf16[512,512]{1,0:T(8,128)(2,1)S(1)} %project.5.own), channel_id=1, source_target_pairs={{0,16},{8,24},{16,32},{24,40},{32,48},{40,56},{48,64},{56,72},{64,... | collective-permute-start | bytes 1572872 | tf_op jit(solution)/shard_map/ppermute | solution.py:47
  141.5 2.8 %collective-permute-done.17.e1 = bf16[512,512]{1,0:T(8,128)(2,1)S(1)} collective-permute-done((bf16[512,512]{1,0:T(8,128)(2,1)S(1)}, bf16[512,512]{1,0:T(8,128)(2,1)S(1)}, u32[]{:S(2)}, u32[]{:S(2)}) %collective-permute-start.17) | collective-permute-done | bytes 524320 | tf_op jit(solution)/shard_map/ppermute | solution.py:47
  146.6 12.5 %collective-permute-done.16.e2 = bf16[512,512]{1,0:T(8,128)(2,1)S(1)} collective-permute-done((bf16[512,512]{1,0:T(8,128)(2,1)S(1)}, bf16[512,512]{1,0:T(8,128)(2,1)S(1)}, u32[]{:S(2)}, u32[]{:S(2)}) %collective-permute-start.16) | collective-permute-done | bytes 524320 | tf_op jit(solution)/shard_map/ppermute | solution.py:47
  159.1 3.2 %far_scores.1 = (bf16[4,1280,256]{2,1,0:T(8,128)(2,1)S(1)}, f32[512,256]{1,0:T(8,128)S(1)}, bf16[512,256]{1,0:T(8,128)(2,1)S(1)}, bf16[512,256]{1,0:T(8,128)(2,1)S(1)}) custom-call(s32[1,32]{1,0:T(1,128)S(1)} %bitcast.7, bf16[512,512]{1,0:T(8,128)(2,1)S(1)} %project.3.q_ref, bf16[512,512]{1,0:T(8,128)(2,1)S(1)} %collective-permute-done.16.e2, ...), custom_call_target="tpu_custom_call" | custom-call | flops 1006632960 | bytes 15728640 | tf_op jit(solution)/shard_map/far_scores/pallas_call | solution.py:310
  167.9 3.6 %collective-permute-done.18 = bf16[512,256]{1,0:T(8,128)(2,1)S(1)} collective-permute-done((bf16[512,256]{1,0:T(8,128)(2,1)S(1)}, bf16[512,256]{1,0:T(8,128)(2,1)S(1)}, u32[]{:S(2)}, u32[]{:S(2)}) %collective-permute-start.18) | collective-permute-done | bytes 262176 | tf_op jit(solution)/shard_map/ppermute | solution.py:47
  (39 shorter events, 30.2 us)
Async XLA Ops:
  0.6 67.1 %copy-start = (bf16[512,480]{0,1:T(8,128)(2,1)S(1)}, bf16[512,480]{0,1:T(8,128)(2,1)}, u32[]{:S(2)}) copy-start(bf16[512,480]{0,1:T(8,128)(2,1)} %param.6) | copy-start | bytes 1474564
  22.6 16.8 %collective-permute-start.7 = (bf16[8,64,1024]{2,1,0:T(8,128)(2,1)S(1)}, bf16[8,64,1024]{2,1,0:T(8,128)(2,1)S(1)}, u32[]{:S(2)}, u32[]{:S(2)}) collective-permute-start(bf16[8,64,1024]{2,1,0:T(8,128)(2,1)S(1)} %pad.4.w_ref), channel_id=1, source_target_pairs={{0,16},{8,120},{128,144},{136,248},{256,272},{264,376},{384,400},{... | collective-permute-start | bytes 3145736 | tf_op jit(solution)/shard_map/ppermute | solution.py:41
  39.5 11.1 %collective-permute-start.12 = (bf16[8,64,512]{2,1,0:T(8,128)(2,1)S(1)}, bf16[8,64,512]{2,1,0:T(8,128)(2,1)S(1)}, u32[]{:S(2)}, u32[]{:S(2)}) collective-permute-start(bf16[8,64,512]{2,1,0:T(8,128)(2,1)S(1)} %get-tuple-element.16.refs_0_.refs_7_.refs_3_), channel_id=1, source_target_pairs={{0,16},{8,120},{128,144},{136,248},{256,272},{264,376},{384,400},{... | collective-permute-start | bytes 1572872 | tf_op jit(solution)/shard_map/ppermute | solution.py:41
  44.5 11.7 %collective-permute-start.8 = (bf16[8,64,512]{2,1,0:T(8,128)(2,1)S(1)}, bf16[8,64,512]{2,1,0:T(8,128)(2,1)S(1)}, u32[]{:S(2)}, u32[]{:S(2)}) collective-permute-start(bf16[8,64,512]{2,1,0:T(8,128)(2,1)S(1)} %get-tuple-element.14.refs_0_.refs_9_), channel_id=1, source_target_pairs={{0,16},{8,120},{128,144},{136,248},{256,272},{264,376},{384,400},{... | collective-permute-start | bytes 1572872 | tf_op jit(solution)/shard_map/ppermute | solution.py:41
  50.6 11.2 %collective-permute-start.13 = (bf16[8,64,512]{2,1,0:T(8,128)(2,1)S(1)}, bf16[8,64,512]{2,1,0:T(8,128)(2,1)S(1)}, u32[]{:S(2)}, u32[]{:S(2)}) collective-permute-start(bf16[8,64,512]{2,1,0:T(8,128)(2,1)S(1)} %collective-permute-done.12.refs_1_.refs_8_.refs_4_), channel_id=1, source_target_pairs={{0,16},{8,120},{128,144},{136,248},{256,272},{264,376},{384,400},{... | collective-permute-start | bytes 1572872 | tf_op jit(solution)/shard_map/ppermute | solution.py:41
  56.2 26.6 %collective-permute-start.9 = (bf16[8,64,512]{2,1,0:T(8,128)(2,1)S(1)}, bf16[8,64,512]{2,1,0:T(8,128)(2,1)S(1)}, u32[]{:S(2)}, u32[]{:S(2)}) collective-permute-start(bf16[8,64,512]{2,1,0:T(8,128)(2,1)S(1)} %collective-permute-done.8.refs_1_.refs_10_), channel_id=1, source_target_pairs={{0,16},{8,120},{128,144},{136,248},{256,272},{264,376},{384,400},{... | collective-permute-start | bytes 1572872 | tf_op jit(solution)/shard_map/ppermute | solution.py:41
  62.0 62.7 %collective-permute-start.15 = (bf16[24,64,512]{2,1,0:T(8,128)(2,1)S(1)}, bf16[24,64,512]{2,1,0:T(8,128)(2,1)S(1)}, u32[]{:S(2)}, u32[]{:S(2)}) collective-permute-start(bf16[24,64,512]{2,1,0:T(8,128)(2,1)S(1)} %join.3), channel_id=1, source_target_pairs={{0,8},{8,0},{128,136},{136,128},{256,264},{264,256},{384,392},{392... | collective-permute-start | bytes 4718600 | tf_op jit(solution)/shard_map/ppermute | solution.py:41
  68.3 31.5 %collective-permute-start.3 = (bf16[512,512]{1,0:T(8,128)(2,1)S(1)}, bf16[512,512]{1,0:T(8,128)(2,1)S(1)}, u32[]{:S(2)}, u32[]{:S(2)}) collective-permute-start(bf16[512,512]{1,0:T(8,128)(2,1)S(1)} %fusion.refs_0_), channel_id=1, source_target_pairs={{0,1},{8,9},{128,129},{136,137},{256,257},{264,265},{384,385},{392... | collective-permute-start | bytes 1572872 | tf_op jit(solution)/shard_map/ppermute | solution.py:41
  76.3 26.7 %collective-permute-start.2 = (bf16[512,512]{1,0:T(8,128)(2,1)S(1)}, bf16[512,512]{1,0:T(8,128)(2,1)S(1)}, u32[]{:S(2)}, u32[]{:S(2)}) collective-permute-start(bf16[512,512]{1,0:T(8,128)(2,1)S(1)} %fusion.refs_0_), channel_id=1, source_target_pairs={{0,6},{8,10},{128,134},{136,138},{256,262},{264,266},{384,390},{39... | collective-permute-start | bytes 1572872 | tf_op jit(solution)/shard_map/ppermute | solution.py:41
  79.4 26.9 %collective-permute-start = (bf16[512,512]{1,0:T(8,128)(2,1)S(1)}, bf16[512,512]{1,0:T(8,128)(2,1)S(1)}, u32[]{:S(2)}, u32[]{:S(2)}) collective-permute-start(bf16[512,512]{1,0:T(8,128)(2,1)S(1)} %fusion.refs_0_), channel_id=1, source_target_pairs={{0,2},{8,14},{128,130},{136,142},{256,258},{264,270},{384,386},{39... | collective-permute-start | bytes 1572872 | tf_op jit(solution)/shard_map/ppermute | solution.py:41
  82.9 56.1 %collective-permute-start.11 = (bf16[24,64,512]{2,1,0:T(8,128)(2,1)S(1)}, bf16[24,64,512]{2,1,0:T(8,128)(2,1)S(1)}, u32[]{:S(2)}, u32[]{:S(2)}) collective-permute-start(bf16[24,64,512]{2,1,0:T(8,128)(2,1)S(1)} %join.2), channel_id=1, source_target_pairs={{0,8},{8,0},{128,136},{136,128},{256,264},{264,256},{384,392},{392... | collective-permute-start | bytes 4718600 | tf_op jit(solution)/shard_map/ppermute | solution.py:41
  99.8 11.1 %collective-permute-start.6 = (bf16[512,512]{1,0:T(8,128)(2,1)S(1)}, bf16[512,512]{1,0:T(8,128)(2,1)S(1)}, u32[]{:S(2)}, u32[]{:S(2)}) collective-permute-start(bf16[512,512]{1,0:T(8,128)(2,1)S(1)} %collective-permute-done.3.refs_4_.refs_3_), channel_id=1, source_target_pairs={{0,6},{8,10},{128,134},{136,138},{256,262},{264,266},{384,390},{39... | collective-permute-start | bytes 1572872 | tf_op jit(solution)/shard_map/ppermute | solution.py:41
  103.0 14.3 %collective-permute-start.4 = (bf16[512,512]{1,0:T(8,128)(2,1)S(1)}, bf16[512,512]{1,0:T(8,128)(2,1)S(1)}, u32[]{:S(2)}, u32[]{:S(2)}) collective-permute-start(bf16[512,512]{1,0:T(8,128)(2,1)S(1)} %collective-permute-done.3.refs_4_.refs_3_), channel_id=1, source_target_pairs={{0,2},{8,14},{128,130},{136,142},{256,258},{264,270},{384,386},{39... | collective-permute-start | bytes 1572872 | tf_op jit(solution)/shard_map/ppermute | solution.py:41
  106.4 16.3 %collective-permute-start.14 = (bf16[8,64,512]{2,1,0:T(8,128)(2,1)S(1)}, bf16[8,64,512]{2,1,0:T(8,128)(2,1)S(1)}, u32[]{:S(2)}, u32[]{:S(2)}) collective-permute-start(bf16[8,64,512]{2,1,0:T(8,128)(2,1)S(1)} %collective-permute-done.13.refs_2_.refs_9_.refs_5_), channel_id=1, source_target_pairs={{0,16},{8,120},{128,144},{136,248},{256,272},{264,376},{384,400},{... | collective-permute-start | bytes 1572872 | tf_op jit(solution)/shard_map/ppermute | solution.py:41
  111.0 15.5 %collective-permute-start.1 = (bf16[512,512]{1,0:T(8,128)(2,1)S(1)}, bf16[512,512]{1,0:T(8,128)(2,1)S(1)}, u32[]{:S(2)}, u32[]{:S(2)}) collective-permute-start(bf16[512,512]{1,0:T(8,128)(2,1)S(1)} %collective-permute-done.refs_1_), channel_id=1, source_target_pairs={{0,2},{8,14},{128,130},{136,142},{256,258},{264,270},{384,386},{39... | collective-permute-start | bytes 1572872 | tf_op jit(solution)/shard_map/ppermute | solution.py:41
  117.3 11.4 %collective-permute-start.5 = (bf16[512,512]{1,0:T(8,128)(2,1)S(1)}, bf16[512,512]{1,0:T(8,128)(2,1)S(1)}, u32[]{:S(2)}, u32[]{:S(2)}) collective-permute-start(bf16[512,512]{1,0:T(8,128)(2,1)S(1)} %collective-permute-done.4.refs_5_.refs_4_), channel_id=1, source_target_pairs={{0,2},{8,14},{128,130},{136,142},{256,258},{264,270},{384,386},{39... | collective-permute-start | bytes 1572872 | tf_op jit(solution)/shard_map/ppermute | solution.py:41
  122.7 16.4 %collective-permute-start.10 = (bf16[8,64,512]{2,1,0:T(8,128)(2,1)S(1)}, bf16[8,64,512]{2,1,0:T(8,128)(2,1)S(1)}, u32[]{:S(2)}, u32[]{:S(2)}) collective-permute-start(bf16[8,64,512]{2,1,0:T(8,128)(2,1)S(1)} %collective-permute-done.9.refs_2_.refs_11_), channel_id=1, source_target_pairs={{0,16},{8,120},{128,144},{136,248},{256,272},{264,376},{384,400},{... | collective-permute-start | bytes 1572872 | tf_op jit(solution)/shard_map/ppermute | solution.py:41
  129.4 14.9 %collective-permute-start.17 = (bf16[512,512]{1,0:T(8,128)(2,1)S(1)}, bf16[512,512]{1,0:T(8,128)(2,1)S(1)}, u32[]{:S(2)}, u32[]{:S(2)}) collective-permute-start(bf16[512,512]{1,0:T(8,128)(2,1)S(1)} %project.5.own), channel_id=1, source_target_pairs={{0,8},{8,16},{16,24},{24,32},{32,40},{40,48},{48,56},{56,64},{64,7... | collective-permute-start | bytes 1572872 | tf_op jit(solution)/shard_map/ppermute | solution.py:47
  136.3 22.8 %collective-permute-start.16 = (bf16[512,512]{1,0:T(8,128)(2,1)S(1)}, bf16[512,512]{1,0:T(8,128)(2,1)S(1)}, u32[]{:S(2)}, u32[]{:S(2)}) collective-permute-start(bf16[512,512]{1,0:T(8,128)(2,1)S(1)} %project.5.own), channel_id=1, source_target_pairs={{0,16},{8,24},{16,32},{24,40},{32,48},{40,56},{48,64},{56,72},{64,... | collective-permute-start | bytes 1572872 | tf_op jit(solution)/shard_map/ppermute | solution.py:47
  139.1 5.3 %copy-start.1 = (bf16[512,512]{1,0:T(8,128)(2,1)S(1)}, bf16[512,512]{1,0:T(8,128)(2,1)}, u32[]{:S(2)}) copy-start(bf16[512,512]{1,0:T(8,128)(2,1)} %g_ref.3) | copy-start | bytes 1572868
  139.1 5.3 %copy-start.2 = (s32[32]{0:T(128)S(1)}, s32[32]{0:T(128)}, u32[]{:S(2)}) copy-start(s32[32]{0:T(128)} %param.11) | copy-start | bytes 388
  162.4 9.1 %collective-permute-start.18 = (bf16[512,256]{1,0:T(8,128)(2,1)S(1)}, bf16[512,256]{1,0:T(8,128)(2,1)S(1)}, u32[]{:S(2)}, u32[]{:S(2)}) collective-permute-start(bf16[512,256]{1,0:T(8,128)(2,1)S(1)} %get-tuple-element.22), channel_id=1, source_target_pairs={{16,0},{24,8},{32,16},{40,24},{48,32},{56,40},{64,48},{72,56},{80,... | collective-permute-start | bytes 786440 | tf_op jit(solution)/shard_map/ppermute | solution.py:47
  164.3 8.8 %collective-permute-start.19 = (bf16[512,256]{1,0:T(8,128)(2,1)S(1)}, bf16[512,256]{1,0:T(8,128)(2,1)S(1)}, u32[]{:S(2)}, u32[]{:S(2)}) collective-permute-start(bf16[512,256]{1,0:T(8,128)(2,1)S(1)} %get-tuple-element.23), channel_id=1, source_target_pairs={{8,0},{16,8},{24,16},{32,24},{40,32},{48,40},{56,48},{64,56},{72,6... | collective-permute-start | bytes 786440 | tf_op jit(solution)/shard_map/ppermute | solution.py:47
